TPU v7x, 256 devices: a whole 4x4x8 slice. The times are simulated.
256 devices in a mesh: space: 32 (over y, z), frag: 8 (over x, core).
Axes of the slice: x: 4, y: 4, z: 8, core: 2. Of those that a mesh axis runs over, the one named last changes fastest.
Arguments:
- latents: bfloat16 [1048576, 128], P(('space', 'frag')), may hold values from -6 to 6
- positions: float32 [3, 1048576], P(None, ('space', 'frag')), may hold values from 0 to 12
- masses: float32 [1048576], P(('space', 'frag')), may hold values from 0.5 to 2
- w_value: bfloat16 [128, 128], replicated, may hold values from -0.5 to 0.5
- w_self: bfloat16 [128, 128], replicated, may hold values from -0.5 to 0.5
- w_message: bfloat16 [128, 128], replicated, may hold values from -0.5 to 0.5
- w_offset: float32 [3, 128], replicated, may hold values from -3.5 to 3.5
- bias_hidden: float32 [128], replicated, may hold values from -3 to 3
- w_out: bfloat16 [128, 128], replicated, may hold values from -0.5 to 0.5
- norm_gain: float32 [128], replicated, may hold values from 0.1 to 1.9
- tile_blocks: int32 [2, 163840], P(None, ('space', 'frag')), may hold values from 0 to 39, as said below
- tile_count: int32 [256], P(('space', 'frag')), may hold values from 80 to 640, as said below
- send_rows: int32 [4, 65536], P(None, ('space', 'frag')), may hold values from 0 to 4095
- frag_ids: int32 [1048576], P(('space', 'frag')), may hold values from 0 to 1023
Outputs:
- updated: bfloat16 [1048576, 128], P(('space', 'frag'))
- pooled: float32 [1024, 128], P('frag')
Inputs may be any that keep to these rules, and one draw needn't show every extreme that they name: `tile_blocks`: row 0 names a block of the device's own 32 blocks; row 1 names one of the 40 blocks of the extended rows. Only the first tile_count slots of a device are live; some device has all 640 live.
All inputs are finite; a program needn't handle non-finite values.
Results may differ from a plain program's by a relative error of at most 0.012.
Values may be sent and summed in bfloat16 or wider, within the bound.
A program may use at most 64 MiB of HBM per device.

v0:
```python
import math

import jax
import jax.numpy as jnp
from jax import lax
from jax.sharding import PartitionSpec as P

D = 128
TILE = 128
GROUP = 32
REACH = 2
FR_DEV = 128


norm_eps = 1e-05


def passed_along(value, axis, by):
    size = lax.axis_size(axis)
    pairs = [(i, i + by) for i in range(size) if 0 <= i + by < size]
    return lax.ppermute(value, axis, pairs)


def offsets_list():
    return [shift_by for shift_by in range(-REACH, REACH + 1) if shift_by != 0]


def tile_terms(running, group_id, blocks, live_tiles, ext_values, ext_pos, ext_mass, recv_blocks):
    message, moment, weight_sum = running
    first_slot = group_id * GROUP
    tile_index = first_slot + jnp.arange(GROUP, dtype=jnp.int32)
    receiver = lax.dynamic_slice_in_dim(blocks[0], first_slot, GROUP, 0)
    sender = lax.dynamic_slice_in_dim(blocks[1], first_slot, GROUP, 0)
    active = (tile_index < live_tiles).astype(jnp.float32)
    recv_pos = recv_blocks[receiver]
    send_pos = ext_pos[sender]
    squared = jnp.zeros((GROUP, TILE, TILE), jnp.float32)
    for c in range(3):
        delta = recv_pos[:, c, :, None] - send_pos[:, c, None, :]
        squared = squared + delta * delta
    distance = jnp.sqrt(squared)
    weight = (ext_mass[sender] * active[:, None])[:, None, :] * jnp.exp(-distance)
    terms = jnp.einsum(
        "gij,gjd->gid",
        weight.astype(jnp.bfloat16),
        ext_values[sender],
        preferred_element_type=jnp.float32,
    )
    message = message.at[receiver].add(terms)
    moment = moment.at[receiver].add(
        jnp.einsum("gij,gcj->gci", weight, send_pos, precision=lax.Precision.HIGHEST)
    )
    weight_sum = weight_sum.at[receiver].add(jnp.sum(weight, axis=2))
    return (message, moment, weight_sum)


def node_update(
    own_latents,
    own_pos,
    message,
    moment,
    weight_sum,
    w_self,
    w_message,
    w_offset,
    bias_hidden,
    w_out,
    norm_gain,
):
    rows = own_latents.shape[0]
    flat_sum = weight_sum.reshape(rows)
    aggregated = (message.reshape(rows, D) * lax.rsqrt(flat_sum)[:, None]).astype(jnp.bfloat16)
    centre = moment.transpose(1, 0, 2).reshape(3, rows) / flat_sum[None, :] - own_pos
    hidden_pre = jnp.dot(own_latents, w_self, preferred_element_type=jnp.float32)
    hidden_pre = hidden_pre + jnp.dot(aggregated, w_message, preferred_element_type=jnp.float32)
    for c in range(3):
        hidden_pre = hidden_pre + centre[c][:, None] * w_offset[c][None, :]
    hidden = jax.nn.silu(hidden_pre + bias_hidden[None, :]).astype(jnp.bfloat16)
    projected = jnp.dot(hidden, w_out, preferred_element_type=jnp.float32)
    row_mean = jnp.mean(projected, axis=1, keepdims=True)
    centred = projected - row_mean
    row_var = jnp.mean(centred * centred, axis=1, keepdims=True)
    normed = centred * lax.rsqrt(row_var + norm_eps) * norm_gain[None, :]
    return (own_latents.astype(jnp.float32) + normed).astype(jnp.bfloat16)


def shards(
    latents,
    positions,
    masses,
    w_value,
    w_self,
    w_message,
    w_offset,
    bias_hidden,
    w_out,
    norm_gain,
    tile_blocks,
    tile_count,
    send_rows,
    frag_ids,
):
    own_rows = latents.shape[0]
    num_blocks = own_rows // TILE
    values = jnp.dot(latents, w_value, preferred_element_type=jnp.float32).astype(jnp.bfloat16)
    shifts_by = offsets_list()
    send_values = values[send_rows]
    send_pos = positions[:, send_rows].transpose(1, 0, 2)
    send_mass = masses[send_rows]
    arrived_by_slot = {}
    for k, shift_by in enumerate(shifts_by):
        arrived_by_slot[k] = (
            passed_along(send_values[k], "space", shift_by),
            passed_along(send_pos[k].astype(jnp.bfloat16), "space", shift_by).astype(jnp.float32),
            passed_along(send_mass[k].astype(jnp.bfloat16), "space", shift_by).astype(jnp.float32),
        )
    halo_values = [values] + [arrived_by_slot[k][0] for k in range(len(shifts_by))]
    halo_pos = [positions] + [arrived_by_slot[k][1] for k in range(len(shifts_by))]
    halo_mass = [masses] + [arrived_by_slot[k][2] for k in range(len(shifts_by))]
    ext_values = jnp.concatenate(halo_values, 0).reshape(-1, TILE, D)
    ext_pos = jnp.concatenate(halo_pos, 1).reshape(3, -1, TILE).transpose(1, 0, 2)
    ext_mass = jnp.concatenate(halo_mass, 0).reshape(-1, TILE)
    recv_blocks = positions.reshape(3, num_blocks, TILE).transpose(1, 0, 2)
    live_tiles = tile_count[0]
    initial = (
        jnp.zeros((num_blocks, TILE, D), jnp.float32),
        recv_blocks * masses.reshape(num_blocks, 1, TILE),
        masses.reshape(num_blocks, TILE),
    )

    def advance(group_id, running):
        return tile_terms(
            running, group_id, tile_blocks, live_tiles, ext_values, ext_pos, ext_mass, recv_blocks
        )

    final = lax.fori_loop(0, tile_blocks.shape[1] // GROUP, advance, initial)
    message, moment, weight_sum = final
    updated = node_update(
        latents,
        positions,
        message,
        moment,
        weight_sum,
        w_self,
        w_message,
        w_offset,
        bias_hidden,
        w_out,
        norm_gain,
    )
    n_space = lax.axis_size("space")
    n_frag = lax.axis_size("frag")
    num_frags = FR_DEV * n_frag
    pool_scale = math.sqrt(num_frags / (own_rows * n_space * n_frag))
    partial_value = jax.ops.segment_sum(
        updated.astype(jnp.float32), frag_ids, num_segments=num_frags
    )
    summed = lax.psum(partial_value.astype(jnp.bfloat16), "space")
    pooled = lax.psum_scatter(summed, "frag", scatter_dimension=0, tiled=True).astype(jnp.float32)
    return (updated, pooled * pool_scale)


def solution(mesh):
    return jax.shard_map(
        shards,
        mesh=mesh,
        in_specs=(
            P(("space", "frag"), None),
            P(None, ("space", "frag")),
            P(("space", "frag")),
            P(),
            P(),
            P(),
            P(),
            P(),
            P(),
            P(),
            P(None, ("space", "frag")),
            P(("space", "frag")),
            P(None, ("space", "frag")),
            P(("space", "frag")),
        ),
        out_specs=(P(("space", "frag"), None), P("frag", None)),
        check_vma=False,
    )
```

profile of v0, /device:TPU:2, one launch (start us, length us, event | category | flops | bytes accessed | tf_op | source)
XLA Modules:
  0.0 1035.6 jit_solution(7022390476027426565)
XLA Ops:
  8.7 6.1 gather_fusion.4
  18.0 5.1 collective-permute-start.2
  23.1 5.8 collective-permute-start.3
  47.9 5.7 collective-permute-start.10
  54.2 5.4 collective-permute-start.11
  62.2 5.7 collective-permute-done.4
  79.2 7.5 collective-permute-start.7
  88.7 727.9 %while.17 = (s32[]{:T(128)}, f32[32,128,128]{2,1,0:T(8,128)S(1)}, f32[32,3,128]{2,1,0:T(4,128)}, f32[32,128]{1,0:T(8,128)S(1)}, s32[2,640]{1,0:T(2,128)}, /*inde...) while((s32[]{:T(128)}, f32[32,128,128]{2,1,0:T(8,128)S(1)}, ...), condition=%wide.region_5.0_spmd, body=%wide.region_0.0_spmd.sunk | while | flops 170412320 | bytes 12668991 | solution.py:136
  105.2 4.7 scatter_fusion
  109.9 6.2 fusion.74
  141.6 4.7 scatter_fusion
  146.3 6.2 fusion.74
  178.0 4.7 scatter_fusion
  182.7 6.2 fusion.74
  219.1 6.2 fusion.74
  250.8 4.7 scatter_fusion
  255.5 6.2 fusion.74
  287.2 4.7 scatter_fusion
  291.9 6.2 fusion.74
  323.6 4.7 scatter_fusion
  328.3 6.2 fusion.74
  360.0 4.7 scatter_fusion
  364.7 6.2 fusion.74
  396.4 4.7 scatter_fusion
  401.1 6.2 fusion.74
  432.8 4.7 scatter_fusion
  437.5 6.2 fusion.74
  469.2 4.7 scatter_fusion
  473.9 6.2 fusion.74
  505.6 4.7 scatter_fusion
  510.2 6.2 fusion.74
  542.0 4.7 scatter_fusion
  546.6 6.2 fusion.74
  578.4 4.7 scatter_fusion
  583.0 6.2 fusion.74
  619.4 6.2 fusion.74
  651.1 4.7 scatter_fusion
  655.8 6.2 fusion.74
  687.5 4.7 scatter_fusion
  692.2 6.2 fusion.74
  728.6 6.2 fusion.74
  760.3 4.7 scatter_fusion
  765.0 6.2 fusion.74
  796.7 4.7 scatter_fusion
  801.4 6.2 fusion.74
  824.8 23.2 %scatter_custom_fusion.3 = f32[1024,128]{1,0:T(8,128)} fusion(s32[4096]{0:T(1024)} %param.29, f32[4096,128]{1,0:T(8,128)S(1)} %copy.23, f32[]{:T(128)} %constant.62.clone.1), kind=kCustom, calls=%fused_computation.58 | custom fusion | flops 524288 | bytes 524800 | tf_op jit(solution)/shard_map/scatter-add | solution.py:155
  851.1 33.8 %reduce-scatter.2.cloned.1.call-done = bf16[128,128]{1,0:T(8,128)(2,1)} async-done(((bf16[1024,128]{1,0:T(8,128)(2,1)}), bf16[128,128]{1,0:T(8,128)(2,1)}) %reduce-scatter.2.cloned.1.call-update) | async-done | bytes 32784 | tf_op jit(solution)/shard_map/reduce_scatter | solution.py:159
  884.9 143.1 %psum.8 = bf16[128,128]{1,0:T(8,128)(2,1)S(1)} all-reduce(bf16[128,128]{1,0:T(8,128)(2,1)} %reduce-scatter.2.cloned.1.call-done), channel_id=1, replica_groups=mesh['space'=32,'frag'=8] {'space'}, use_global_device_ids=true, to_apply=%region_9.10 | all-reduce | flops 16384 | bytes 65536 | tf_op jit(solution)/shard_map/psum | solution.py:158
  (409 shorter events, 575.3 us)
Async XLA Ops:
  7.2 21.7 %copy-start = (bf16[128,128]{1,0:T(8,128)(2,1)S(1)}, bf16[128,128]{1,0:T(8,128)(2,1)}, u32[]{:S(2)}) copy-start(bf16[128,128]{1,0:T(8,128)(2,1)} %param.19) | copy-start | bytes 98308
  7.2 21.7 %copy-start.1 = (bf16[4096,128]{1,0:T(8,128)(2,1)S(1)}, bf16[4096,128]{1,0:T(8,128)(2,1)}, u32[]{:S(2)}) copy-start(bf16[4096,128]{1,0:T(8,128)(2,1)} %param.16) | copy-start | bytes 3145732
  7.2 877.8 %reduce-scatter.2.cloned.1.call-start = ((), (), s32[]{:S(2)}) async-start(), calls=%async_computation.1 | async-start | bytes 294912 | tf_op jit(solution)/shard_map/reduce_scatter | solution.py:159
  15.4 30.6 %collective-permute-start = (bf16[256]{0:T(256)(128)(2,1)}, bf16[256]{0:T(256)(128)(2,1)}, u32[]{:S(2)}, u32[]{:S(2)}) collective-permute-start(bf16[256]{0:T(256)(128)(2,1)} %get-tuple-element.226), channel_id=1, source_target_pairs={{16,0},{24,8},{32,16},{40,24},{48,32},{56,40},{64,48},{72,56},{80,... | collective-permute-start | bytes 1544 | tf_op jit(solution)/shard_map/ppermute | solution.py:21
  16.7 31.2 %collective-permute-start.1 = (bf16[256]{0:T(256)(128)(2,1)S(1)}, bf16[256]{0:T(256)(128)(2,1)}, u32[]{:S(2)}, u32[]{:S(2)}) collective-permute-start(bf16[256]{0:T(256)(128)(2,1)S(1)} %get-tuple-element.225), channel_id=1, source_target_pairs={{8,0},{16,8},{24,16},{32,24},{40,32},{48,40},{56,48},{64,56},{72,6... | collective-permute-start | bytes 1544 | tf_op jit(solution)/shard_map/ppermute | solution.py:21
  18.0 36.2 %collective-permute-start.2 = (bf16[256]{0:T(256)(128)(2,1)S(1)}, bf16[256]{0:T(256)(128)(2,1)}, u32[]{:S(2)}, u32[]{:S(2)}) collective-permute-start(bf16[256]{0:T(256)(128)(2,1)S(1)} %get-tuple-element.227), channel_id=1, source_target_pairs={{0,8},{8,16},{16,24},{24,32},{32,40},{40,48},{48,56},{56,64},{64,7... | collective-permute-start | bytes 1544 | tf_op jit(solution)/shard_map/ppermute | solution.py:21
  23.1 37.2 %collective-permute-start.3 = (bf16[256]{0:T(256)(128)(2,1)S(1)}, bf16[256]{0:T(256)(128)(2,1)}, u32[]{:S(2)}, u32[]{:S(2)}) collective-permute-start(bf16[256]{0:T(256)(128)(2,1)S(1)} %get-tuple-element.224), channel_id=1, source_target_pairs={{0,16},{8,24},{16,32},{24,40},{32,48},{40,56},{48,64},{56,72},{64,... | collective-permute-start | bytes 1544 | tf_op jit(solution)/shard_map/ppermute | solution.py:21
  29.3 6.6 copy-start.2
  29.3 13.1 %copy-start.6 = (f32[3,128]{1,0:T(4,128)S(1)}, f32[3,128]{1,0:T(4,128)}, u32[]{:S(2)}) copy-start(f32[3,128]{1,0:T(4,128)} %param.22) | copy-start | bytes 4612
  33.6 9.3 copy-start.5
  34.6 53.2 %collective-permute-start.8 = (bf16[256,128]{1,0:T(8,128)(2,1)S(1)}, bf16[256,128]{1,0:T(8,128)(2,1)S(1)}, u32[]{:S(2)}, u32[]{:S(2)}) collective-permute-start(bf16[256,128]{1,0:T(8,128)(2,1)S(1)} %get-tuple-element.213), channel_id=1, source_target_pairs={{16,0},{24,8},{32,16},{40,24},{48,32},{56,40},{64,48},{72,56},{80,... | collective-permute-start | bytes 196616 | tf_op jit(solution)/shard_map/ppermute | solution.py:21
  46.0 41.8 %collective-permute-start.9 = (bf16[256,128]{1,0:T(8,128)(2,1)S(1)}, bf16[256,128]{1,0:T(8,128)(2,1)S(1)}, u32[]{:S(2)}, u32[]{:S(2)}) collective-permute-start(bf16[256,128]{1,0:T(8,128)(2,1)S(1)} %get-tuple-element.212), channel_id=1, source_target_pairs={{8,0},{16,8},{24,16},{32,24},{40,32},{48,40},{56,48},{64,56},{72,6... | collective-permute-start | bytes 196616 | tf_op jit(solution)/shard_map/ppermute | solution.py:21
  47.9 40.0 %collective-permute-start.10 = (bf16[256,128]{1,0:T(8,128)(2,1)S(1)}, bf16[256,128]{1,0:T(8,128)(2,1)S(1)}, u32[]{:S(2)}, u32[]{:S(2)}) collective-permute-start(bf16[256,128]{1,0:T(8,128)(2,1)S(1)} %get-tuple-element.211), channel_id=1, source_target_pairs={{0,8},{8,16},{16,24},{24,32},{32,40},{40,48},{48,56},{56,64},{64,7... | collective-permute-start | bytes 196616 | tf_op jit(solution)/shard_map/ppermute | solution.py:21
  54.2 33.7 %collective-permute-start.11 = (bf16[256,128]{1,0:T(8,128)(2,1)S(1)}, bf16[256,128]{1,0:T(8,128)(2,1)S(1)}, u32[]{:S(2)}, u32[]{:S(2)}) collective-permute-start(bf16[256,128]{1,0:T(8,128)(2,1)S(1)} %get-tuple-element.210), channel_id=1, source_target_pairs={{0,16},{8,24},{16,32},{24,40},{32,48},{40,56},{48,64},{56,72},{64,... | collective-permute-start | bytes 196616 | tf_op jit(solution)/shard_map/ppermute | solution.py:21
  60.3 7.6 collective-permute-start.4
  67.8 5.5 collective-permute-start.5
  73.3 5.9 collective-permute-start.6
  79.2 8.7 collective-permute-start.7
  87.8 0.6 copy-start.4
  816.6 2.4 copy-start.8
  816.6 2.4 copy-start.9
  816.6 2.4 copy-start.10
  822.6 1.2 copy-start.3
  822.6 1.2 copy-start.7
Sparse Core Ops, SparseCore 0:
  850.0 34.9 reduce-scatter.1
where the time goes:
time: 1050 us; the launch traced here: 1040 us
  other arithmetic  347 us (33%)
  local copies, waits for them, and re-layouts  227 us (22%)
  matrix products  214 us (20%)
  blocking collectives  143 us (14%)
  waiting for transfers between devices  46.1 us (4%)
  starting transfers between devices  41.8 us (4%)
  between operations  14.4 us (1%)
    psum x1, blocking collectives, shards(): summed = lax.psum(partial_value.astype(jnp.bfloat16), 'space')  143 us
    dot_general x20, matrix products, tile_terms(): jnp.einsum('gij,gcj->gci', weight, send_pos, precision=lax.Precision.HIGH...  124 us
    scatter-add x20, other arithmetic, tile_terms(): message = message.at[receiver].add(terms)  93.4 us
    dot_general x20, matrix products, tile_terms(): jnp.einsum('gij,gjd->gid', weight.astype(jnp.bfloat16), ext_values[sender...  84.6 us
    reduce_sum x20, other arithmetic, tile_terms(): weight_sum = weight_sum.at[receiver].add(jnp.sum(weight, axis=2))  81.6 us
    scatter-add x20, other arithmetic, tile_terms(): moment.at[receiver]  79.9 us
    slice x40, local copies, waits for them, and re-layouts, tile_terms(): delta = recv_pos[:, c, :, None] - send_pos[:, c, None, :]  64.4 us
    gather x20, local copies, waits for them, and re-layouts, tile_terms(): send_pos = ext_pos[sender]  42.3 us
  transfers between devices with their start and end apart: 13, of which 5 were waited for; matrix products, arithmetic and copies ran while one was open for 2% of the time, Pallas kernels for 0%

commit v1 on v0

v1 whole, which is shorter than its diff:
```python
import functools
import math

import jax
import jax.numpy as jnp
import numpy as np
from jax import lax
from jax.experimental import pallas as pl
from jax.experimental.pallas import tpu as pltpu
from jax.sharding import PartitionSpec as P

D = 128
TILE = 128
REACH = 2
HALO = 256
BLOCKS = 32
EXT = 40
NODE = BLOCKS * TILE
SLOTS = 640
FR_DEV = 128
OFFSETS = tuple(o for o in range(-REACH, REACH + 1) if o != 0)
LOG2E = math.log2(math.e)
CENTRE = 6.0
GROUP = 2
UNROLL = 8
NONE = -1e30

f32, bf16, i32 = jnp.float32, jnp.bfloat16, jnp.int32
MESH = pl.DeviceIdType.MESH


def split3(x):
    high = x.astype(bf16).astype(f32)
    rest = x - high
    mid = rest.astype(bf16).astype(f32)
    return high, mid, rest - mid


def feature_maps():
    recv = np.zeros((128, 32), np.float32)
    send = np.zeros((32, 16), np.float32)
    pairs = ((0, 0), (0, 1), (1, 0), (1, 1), (0, 2), (2, 0))
    for p, (a, b) in enumerate(pairs):
        for c in range(3):
            recv[3 * a + c, 3 * p + c] = -2.0
            send[3 * p + c, 3 * b + c] = 1.0
    for c in range(3):
        recv[13 + c, 18 + c] = 1.0
        send[18 + c, 12] = 1.0
        recv[12, 21 + c] = 1.0
        send[21 + c, 13 + c] = 1.0
    return jnp.asarray(recv, bf16), jnp.asarray(send, bf16)


def aux_columns(rows):
    cols = jnp.transpose(rows)
    return jnp.concatenate([cols, jnp.zeros((cols.shape[0], 112), f32)], axis=1).astype(bf16)


def halo_kernel(lat, pos, mass, wv, tb, tc, sr, fa, fb,
                A, B, V, lm, codes, lmult,
                rows_s, hot, sval, saux, rval, raux, ssem, rsem):
    s = lax.axis_index("space")
    f = lax.axis_index("frag")
    n_space = lax.axis_size("space")
    barrier = pltpu.get_barrier_semaphore()
    for o in OFFSETS:
        @pl.when((s + o >= 0) & (s + o < n_space))
        def _():
            pl.semaphore_signal(barrier, inc=1, device_id=(s + o, f), device_id_type=MESH)

    x = (pos[...] - CENTRE) * LOG2E
    xh, xm, xl = split3(x)
    mh, mm, ml = split3(mass[...])
    sq = x * x
    norm = sq[0:1] + sq[1:2] + sq[2:3]
    nh, nm, nl = split3(norm)
    rows = jnp.concatenate([xh, xm, xl, mh, mm, ml, jnp.ones((1, NODE), f32), nh, nm, nl], axis=0)
    rows_s[...] = rows
    for b in range(BLOCKS):
        V[b, :, 128:256] = aux_columns(rows_s[:, b * TILE:(b + 1) * TILE])
    values = jnp.dot(lat[...], wv[...], preferred_element_type=f32).astype(bf16)
    V[0:BLOCKS, :, 0:128] = values.reshape(BLOCKS, TILE, D)

    pl.semaphore_wait(barrier, jnp.minimum(s, REACH) + jnp.minimum(n_space - 1 - s, REACH))

    def copies(k):
        o = OFFSETS[k]
        dev = (s + o, f)
        return (
            pltpu.make_async_remote_copy(
                src_ref=sval.at[k], dst_ref=rval.at[k], send_sem=ssem.at[0, k], recv_sem=rsem.at[0, k],
                device_id=dev, device_id_type=MESH),
            pltpu.make_async_remote_copy(
                src_ref=saux.at[k], dst_ref=raux.at[k], send_sem=ssem.at[1, k], recv_sem=rsem.at[1, k],
                device_id=dev, device_id_type=MESH),
        )

    idx = sr[...].astype(f32)
    idx = jnp.transpose(jnp.concatenate([idx, idx], axis=0))
    lane = lax.broadcasted_iota(i32, (HALO, TILE), 1).astype(f32)
    table = V[0:BLOCKS].reshape(NODE, 256)
    for k in (0, 3, 1, 2):
        col = idx[:, k:k + 1]
        high = jnp.floor(col * (1.0 / TILE))
        low = col - high * TILE
        code = jnp.where(low == lane, high, -1.0).astype(bf16)
        for b in range(BLOCKS):
            hot[:, b * TILE:(b + 1) * TILE] = jnp.where(code == jnp.asarray(b, bf16), 1.0, 0.0).astype(bf16)
        got = jnp.dot(hot[...], table, preferred_element_type=f32)
        sval[k] = got[:, 0:128].astype(bf16)
        saux[k] = jnp.transpose(got[:, 128:256])[0:16].astype(bf16)
        o = OFFSETS[k]

        @pl.when((s + o >= 0) & (s + o < n_space))
        def _():
            for c in copies(k):
                c.start()

        @pl.when((s - o < 0) | (s - o >= n_space))
        def _():
            rval[k] = jnp.zeros((HALO, D), bf16)
            raux[k] = jnp.zeros((16, HALO), bf16)

    A[...] = jnp.dot(V[0:BLOCKS, :, 128:256].reshape(NODE, 128), fa[...],
                     preferred_element_type=f32).astype(bf16).reshape(BLOCKS, TILE, 32)
    rows = rows_s[...]
    own_b = jnp.dot(fb[...], rows.astype(bf16), preferred_element_type=f32).astype(bf16)
    lmass = jnp.log2(mass[...])
    for b in range(BLOCKS):
        B[b] = own_b[:, b * TILE:(b + 1) * TILE]
        lm[b] = lmass[:, b * TILE:(b + 1) * TILE]

    slot = lax.broadcasted_iota(i32, (BLOCKS, SLOTS), 1)
    rhot = (lax.broadcasted_iota(i32, (BLOCKS, SLOTS), 0) == tb[0:1, :]) & (slot < tc[0])
    chot = lax.broadcasted_iota(i32, (128, SLOTS), 0) == tb[1:2, :]
    count = lax.dot_general(
        jnp.where(rhot, 1.0, 0.0).astype(bf16), jnp.where(chot, 1.0, 0.0).astype(bf16),
        (((1,), (1,)), ((), ())), preferred_element_type=f32)
    live = jnp.where(count > 0.0, 1.0, 0.0)
    before = lax.broadcasted_iota(i32, (128, 128), 0) < lax.broadcasted_iota(i32, (128, 128), 1)
    place = jnp.dot(live.astype(bf16), jnp.where(before, 1.0, 0.0).astype(bf16), preferred_element_type=f32)
    place = jnp.where(count > 0.0, place, -1.0)
    col_id = lax.broadcasted_iota(i32, (BLOCKS, 128), 1).astype(f32)
    packed = col_id + 64.0 * count
    listed = jnp.zeros((BLOCKS, 128), f32)
    for c in range(EXT):
        listed = listed + jnp.where(place[:, c:c + 1] == col_id, packed[:, c:c + 1], 0.0)
    times = jnp.floor(listed * (1.0 / 64.0))
    sender = listed - 64.0 * times
    groups = jnp.maximum(jnp.floor((jnp.sum(live, axis=1, keepdims=True) + (GROUP - 1)) * (1.0 / GROUP)), 1.0)
    codes[...] = jnp.where(col_id == 127.0, groups, sender).astype(i32)
    lmult[...] = jnp.where(times > 0.0, jnp.log2(jnp.maximum(times, 1.0)), NONE)

    for k in (0, 3, 1, 2):
        o = OFFSETS[k]

        @pl.when((s - o >= 0) & (s - o < n_space))
        def _():
            for c in copies(k):
                c.wait_recv()

        aux = raux[k].astype(f32)
        V[BLOCKS + 2 * k:BLOCKS + 2 * k + 2, :, 0:128] = rval[k].reshape(2, TILE, D)
        V[BLOCKS + 2 * k:BLOCKS + 2 * k + 2, :, 128:256] = aux_columns(aux).reshape(2, TILE, 128)
        far_b = jnp.dot(fb[...], raux[k], preferred_element_type=f32).astype(bf16)
        far_mass = aux[9:10] + aux[10:11] + aux[11:12]
        far_lm = jnp.where(far_mass > 0.0, jnp.log2(jnp.maximum(far_mass, 1e-30)), NONE)
        for h in range(2):
            B[BLOCKS + 2 * k + h] = far_b[:, h * TILE:(h + 1) * TILE]
            lm[BLOCKS + 2 * k + h] = far_lm[:, h * TILE:(h + 1) * TILE]

    for k in range(4):
        o = OFFSETS[k]

        @pl.when((s + o >= 0) & (s + o < n_space))
        def _():
            for c in copies(k):
                c.wait_send()


def tile_kernel(codes, lmult, A, B, V, lm, lat, w_self, w_message, w_offset, bias, w_out, gain, ids,
                upd, part, acc, wb):
    acc[...] = jnp.zeros_like(acc)
    wb[...] = jnp.zeros_like(wb)
    total = lax.fori_loop(0, BLOCKS, lambda r, t: t + codes[r, 127], 0)

    def advance(state):
        out = []
        for _ in range(UNROLL):
            r, g = state
            over = g + 1 >= codes[r, 127]
            state = (jnp.minimum(jnp.where(over, r + 1, r), BLOCKS - 1), jnp.where(over, 0, g + 1))
            out.append(state)
        return out

    def step(it, states):
        now, last = states[:UNROLL], states[UNROLL:]
        for q in range(UNROLL):
            r, g = last[q]
            sent = jnp.concatenate([V[codes[r, g * GROUP + u]] for u in range(GROUP)], axis=0)
            acc[r] = acc[r] + jnp.dot(wb[q], sent, preferred_element_type=f32)
            r, g = now[q]
            off = jnp.where(it * UNROLL + q < total, 0.0, NONE).astype(f32)
            senders = [codes[r, g * GROUP + u] for u in range(GROUP)]
            sq = jnp.dot(A[r], jnp.concatenate([B[c] for c in senders], axis=1), preferred_element_type=f32)
            for u in range(GROUP):
                level = lm[senders[u]] + (lmult[r, g * GROUP + u] + off)
                d2 = jnp.maximum(sq[:, u * TILE:(u + 1) * TILE], 1e-12)
                wb[q, :, u * TILE:(u + 1) * TILE] = jnp.exp2(level - d2 * lax.rsqrt(d2)).astype(bf16)
        return tuple(advance(now[-1])) + tuple(now)

    zero = jnp.int32(0)
    first = [(zero, zero)] + advance((zero, zero))[:UNROLL - 1]
    lax.fori_loop(0, (total + UNROLL - 1) // UNROLL + 1, step, tuple(first) + ((zero, zero),) * UNROLL)

    ROWS = 512
    row_id = lax.broadcasted_iota(i32, (128, 128), 0)
    mass_map = jnp.where((row_id >= 9) & (row_id < 12), 1.0, 0.0).astype(bf16)
    woff = w_offset[...] * (1.0 / LOG2E)
    wh = woff.astype(bf16).astype(f32)
    wm = woff - wh
    pad = jnp.zeros((119, 128), f32)
    off_h = jnp.concatenate([wh, wh, wh, pad], axis=0).astype(bf16)
    off_m = jnp.concatenate([wm, wm, wm, pad], axis=0).astype(bf16)
    off_hh = jnp.concatenate([off_h, off_h], axis=0)
    w_sm = jnp.concatenate([w_self[...], w_message[...]], axis=0)
    wo = w_out[...].astype(f32)
    wc = wo - jnp.mean(wo, axis=1, keepdims=True)
    wc_h = wc.astype(bf16)
    wc_m = (wc - wc_h.astype(f32)).astype(bf16)
    wc2 = jnp.concatenate([wc_h, wc_m], axis=0)
    bias_row = bias[...]
    gain_row = gain[...]

    def node(i, _):
        blk = ROWS // TILE
        got = acc[pl.ds(i * blk, blk)].reshape(ROWS, 256)
        own_b = V[pl.ds(i * blk, blk), :, 128:256].reshape(ROWS, 128)
        mine = lat[pl.ds(pl.multiple_of(i * ROWS, ROWS), ROWS), :]
        own = own_b.astype(f32)
        m = jnp.dot(own_b, mass_map, preferred_element_type=f32)
        tot = got[:, 128:256] + m * own
        rs = lax.rsqrt(tot[:, 12:13])
        agg = (got[:, 0:128] * rs).astype(bf16)
        q = tot * (rs * rs) - own
        qh = q.astype(bf16)
        qm = (q - qh.astype(f32)).astype(bf16)
        pre = jnp.dot(jnp.concatenate([mine, agg], axis=1), w_sm, preferred_element_type=f32)
        pre = pre + jnp.dot(jnp.concatenate([qh, qm], axis=1), off_hh, preferred_element_type=f32)
        pre = pre + jnp.dot(qh, off_m, preferred_element_type=f32)
        pre = pre + bias_row
        hid = (pre * (0.5 + 0.5 * jnp.tanh(0.5 * pre))).astype(bf16)
        cen = jnp.dot(jnp.concatenate([hid, hid], axis=1), wc2, preferred_element_type=f32)
        var = jnp.mean(cen * cen, axis=1, keepdims=True)
        out = mine.astype(f32) + cen * lax.rsqrt(var + 1e-5) * gain_row
        upd[pl.ds(pl.multiple_of(i * ROWS, ROWS), ROWS), :] = out.astype(bf16)
        return 0

    lax.fori_loop(0, NODE // ROWS, node, 0)

    row = ids[...].astype(f32)
    high = jnp.floor(row * (1.0 / FR_DEV))
    low = row - high * FR_DEV
    sub = lax.broadcasted_iota(i32, (FR_DEV, NODE), 0).astype(f32).astype(bf16)
    for t in range(8):
        want = jnp.where(high == float(t), low, -1.0).astype(bf16)
        hot = jnp.where(jnp.broadcast_to(want, (FR_DEV, NODE)) == sub, 1.0, 0.0).astype(bf16)
        part[t] = jnp.dot(hot, upd[...], preferred_element_type=f32).astype(bf16)


def pool_kernel(scale, part, out, got1, mine, got2, full, s1, r1, s2, r2, s3, r3):
    s = lax.axis_index("space")
    f = lax.axis_index("frag")
    ns = lax.axis_size("space")
    nf = lax.axis_size("frag")
    barrier = pltpu.get_barrier_semaphore()

    def greet_f(i, _):
        pl.semaphore_signal(barrier, inc=1, device_id=(s, lax.rem(f + i, nf)), device_id_type=MESH)
        return 0

    def greet_s(i, _):
        pl.semaphore_signal(barrier, inc=1, device_id=(lax.rem(s + i, ns), f), device_id_type=MESH)
        return 0

    lax.fori_loop(1, nf, greet_f, 0)
    lax.fori_loop(1, ns, greet_s, 0)
    pl.semaphore_wait(barrier, nf + ns - 2)

    def copy1(i):
        to = lax.rem(f + i, nf)
        return pltpu.make_async_remote_copy(
            src_ref=part.at[to], dst_ref=got1.at[i - 1], send_sem=s1.at[i - 1], recv_sem=r1.at[i - 1],
            device_id=(s, to), device_id_type=MESH)

    def copy2(i):
        to = lax.rem(s + i, ns)
        return pltpu.make_async_remote_copy(
            src_ref=mine.at[to], dst_ref=got2.at[i - 1], send_sem=s2.at[i - 1], recv_sem=r2.at[i - 1],
            device_id=(to, f), device_id_type=MESH)

    def copy3(i):
        to = lax.rem(s + i, ns)
        return pltpu.make_async_remote_copy(
            src_ref=full.at[s], dst_ref=full.at[s], send_sem=s3.at[i - 1], recv_sem=r3.at[i - 1],
            device_id=(to, f), device_id_type=MESH)

    def each(n, fn):
        def body(i, _):
            fn(i)
            return 0
        lax.fori_loop(1, n, body, 0)

    each(nf, lambda i: copy1(i).start())
    each(nf, lambda i: copy1(i).wait_recv())
    total = part[f].astype(f32)
    for i in range(nf - 1):
        total = total + got1[i].astype(f32)
    mine[...] = total.reshape(ns, FR_DEV // ns, D)
    each(ns, lambda i: copy2(i).start())
    each(ns, lambda i: copy2(i).wait_recv())
    full[s] = (mine[s] + jnp.sum(got2[...], axis=0)) * scale
    each(ns, lambda i: copy3(i).start())
    each(ns, lambda i: copy3(i).wait_recv())
    out[...] = full[...].reshape(FR_DEV, D)
    each(nf, lambda i: copy1(i).wait_send())
    each(ns, lambda i: copy2(i).wait_send())
    each(ns, lambda i: copy3(i).wait_send())


def shards(latents, positions, masses, w_value, w_self, w_message, w_offset, bias_hidden, w_out, norm_gain,
           tile_blocks, tile_count, send_rows, frag_ids):
    ns, nf = lax.axis_size("space"), lax.axis_size("frag")
    vm = pl.BlockSpec(memory_space=pltpu.VMEM)
    sm = pl.BlockSpec(memory_space=pltpu.SMEM)
    fa, fb = feature_maps()
    dma = pltpu.SemaphoreType.DMA
    A, B, V, lm, codes, lmult = pl.pallas_call(
        halo_kernel,
        out_shape=(
            jax.ShapeDtypeStruct((BLOCKS, TILE, 32), bf16),
            jax.ShapeDtypeStruct((EXT, 32, TILE), bf16),
            jax.ShapeDtypeStruct((EXT, TILE, 256), bf16),
            jax.ShapeDtypeStruct((EXT, 1, TILE), f32),
            jax.ShapeDtypeStruct((BLOCKS, 128), i32),
            jax.ShapeDtypeStruct((BLOCKS, 128), f32),
        ),
        in_specs=[vm] * 5 + [sm] + [vm] * 3,
        out_specs=(vm,) * 6,
        scratch_shapes=[
            pltpu.VMEM((16, NODE), f32),
            pltpu.VMEM((HALO, NODE), bf16),
            pltpu.VMEM((4, HALO, D), bf16),
            pltpu.VMEM((4, 16, HALO), bf16),
            pltpu.VMEM((4, HALO, D), bf16),
            pltpu.VMEM((4, 16, HALO), bf16),
            dma((2, 4)),
            dma((2, 4)),
        ],
        compiler_params=pltpu.CompilerParams(
            collective_id=0, has_side_effects=True, vmem_limit_bytes=40 << 20),
    )(latents, positions, masses.reshape(1, NODE), w_value, tile_blocks, tile_count, send_rows, fa, fb)

    updated, part = pl.pallas_call(
        tile_kernel,
        out_shape=(
            jax.ShapeDtypeStruct((NODE, D), bf16),
            jax.ShapeDtypeStruct((nf, FR_DEV, D), bf16),
        ),
        in_specs=[sm, sm] + [vm] * 12,
        out_specs=(vm, vm),
        scratch_shapes=[
            pltpu.VMEM((BLOCKS, TILE, 256), f32),
            pltpu.VMEM((UNROLL, TILE, GROUP * TILE), bf16),
        ],
        compiler_params=pltpu.CompilerParams(vmem_limit_bytes=40 << 20),
    )(codes, lmult, A, B, V, lm, latents, w_self, w_message, w_offset, bias_hidden.reshape(1, D), w_out,
      norm_gain.reshape(1, D), frag_ids.reshape(1, NODE))

    scale = math.sqrt(FR_DEV * nf / (NODE * ns * nf))
    pooled = pl.pallas_call(
        functools.partial(pool_kernel, scale),
        out_shape=jax.ShapeDtypeStruct((FR_DEV, D), f32),
        in_specs=[vm],
        out_specs=vm,
        scratch_shapes=[
            pltpu.VMEM((nf - 1, FR_DEV, D), bf16),
            pltpu.VMEM((ns, FR_DEV // ns, D), f32),
            pltpu.VMEM((ns - 1, FR_DEV // ns, D), f32),
            pltpu.VMEM((ns, FR_DEV // ns, D), f32),
            dma((nf - 1,)), dma((nf - 1,)),
            dma((ns - 1,)), dma((ns - 1,)),
            dma((ns - 1,)), dma((ns - 1,)),
        ],
        compiler_params=pltpu.CompilerParams(collective_id=1, has_side_effects=True),
    )(part)
    return updated, pooled


def solution(mesh):
    own = P(("space", "frag"))
    return jax.shard_map(
        shards,
        mesh=mesh,
        in_specs=(
            P(("space", "frag"), None), P(None, ("space", "frag")), own,
            P(), P(), P(), P(), P(), P(), P(),
            P(None, ("space", "frag")), own, P(None, ("space", "frag")), own,
        ),
        out_specs=(P(("space", "frag"), None), P("frag", None)),
        check_vma=False,
    )
```

time: 1050 us -> 87.2 us (0.08)
  the two profiles are of different devices: /device:TPU:2 before, /device:TPU:1 now
where the time goes in v1:
time: 87.2 us; the launch traced here: 86.3 us
  Pallas kernels  71.5 us (82%)
  local copies, waits for them, and re-layouts  13.5 us (15%)
  between operations  1.34 us (2%)
    pallas_call x1, Pallas kernels, shards(): pl.pallas_call(functools.partial(pool_kernel, scale), out_shape=jax.Shape...  31.5 us
    pallas_call x1, Pallas kernels, shards(): pl.pallas_call(tile_kernel, out_shape=(jax.ShapeDtypeStruct((NODE, D), bf...  25.5 us
    pallas_call x1, Pallas kernels, shards(): pl.pallas_call(halo_kernel, out_shape=(jax.ShapeDtypeStruct((BLOCKS, TILE...  14.5 us
    unnamed x33, local copies, waits for them, and re-layouts  13.5 us

profile of v1, /device:TPU:1, one launch (start us, length us, event | category | flops | bytes accessed | tf_op | source)
XLA Modules:
  0.0 86.3 jit_solution(3125284915497586221)
XLA Ops:
  1.3 0.0 copy-start
  1.3 1.2 %copy-done = bf16[4096,128]{1,0:T(8,128)(2,1)S(1)} copy-done((bf16[4096,128]{1,0:T(8,128)(2,1)S(1)}, bf16[4096,128]{1,0:T(8,128)(2,1)}, u32[]{:S(2)}) %copy-start) | copy-done | bytes 1048600
  2.5 0.0 copy-start.2
  2.5 0.8 copy-done.2
  3.3 0.0 copy-start.6
  3.3 0.8 copy-done.6
  4.1 0.0 copy-start.7
  4.1 0.8 copy-done.7
  4.9 0.0 copy-start.8
  4.9 0.7 copy-done.8
  5.6 0.0 copy-start.10
  5.6 0.7 copy-done.10
  6.3 0.0 copy-start.11
  6.3 0.7 copy-done.11
  7.0 0.0 copy-start.12
  7.0 0.7 copy-done.12
  7.7 14.5 %shard_map.167 = (bf16[32,128,32]{2,1,0:T(8,128)(2,1)S(1)}, bf16[40,32,128]{2,1,0:T(8,128)(2,1)S(1)}, bf16[40,128,256]{2,1,0:T(8,128)(2,1)S(1)}, f32[40,1,128]{2...) custom-call(bf16[4096,128]{1,0:T(8,128)(2,1)S(1)} %copy-done, f32[3,4096]{1,0:T(4,128)S(1)} %copy-done.2, ...), custom_call_target="tpu_custom_call" | custom-call | tf_op jit(solution)/shard_map/pallas_call | solution.py:339
  22.2 0.0 copy-start.3
  22.2 0.7 copy-done.3
  22.9 0.0 copy-start.4
  22.9 0.8 copy-done.4
  23.7 0.0 copy-start.5
  23.7 0.8 copy-done.5
  24.4 0.0 copy-start.9
  24.4 0.7 copy-done.9
  25.1 0.0 copy-start.13
  25.2 0.7 copy-done.13
  25.8 0.0 copy-start.14
  25.8 0.7 copy-done.14
  26.5 0.0 copy-start.15
  26.5 0.7 copy-done.15
  27.1 25.5 %shard_map.168 = (bf16[4096,128]{1,0:T(8,128)(2,1)}, bf16[8,128,128]{2,1,0:T(8,128)(2,1)S(1)}) custom-call(s32[32,128]{1,0:T(8,128)S(1)} %get-tuple-element.10.codes, f32[32,128]{1,0:T(8,128)S(1)} %get-tuple-element.11.lmult, bf16[32,128,32]{2,1,0:T(8,128)(2,1)S(1)} %get-tuple-element.12.A, bf16[40,32,128]{2,1,0:T(8,128)(2,1)S(1)} %get-tuple-element.13.B, ...), custom_call_target="tpu_custom_call" | custom-call | tf_op jit(solution)/shard_map/pallas_call | solution.py:365
  52.6 0.0 copy-start.1
  52.6 0.7 copy-done.1
  53.3 31.5 %shard_map.169 = f32[128,128]{1,0:T(8,128)} custom-call(bf16[8,128,128]{2,1,0:T(8,128)(2,1)} %copy-done.1), custom_call_target="tpu_custom_call" | custom-call | tf_op jit(solution)/shard_map/pallas_call | solution.py:382
  84.8 1.5 %copy.20 = f32[128,128]{1,0:T(8,128)} copy(f32[128,128]{1,0:T(8,128)} %shard_map.169) | data formatting | bytes 131072
Async XLA Ops:
  1.3 1.2 %copy-start = (bf16[4096,128]{1,0:T(8,128)(2,1)S(1)}, bf16[4096,128]{1,0:T(8,128)(2,1)}, u32[]{:S(2)}) copy-start(bf16[4096,128]{1,0:T(8,128)(2,1)} %lat.3) | copy-start | bytes 3145732
  2.5 0.8 copy-start.2
  3.3 0.8 copy-start.6
  4.1 0.8 copy-start.7
  4.9 0.7 copy-start.8
  5.6 0.7 copy-start.10
  6.3 0.7 copy-start.11
  7.0 0.7 copy-start.12
  22.2 0.8 copy-start.3
  22.9 0.8 copy-start.4
  23.7 0.8 copy-start.5
  24.4 0.7 copy-start.9
  25.1 0.7 copy-start.13
  25.8 0.7 copy-start.14
  26.5 0.7 copy-start.15
  52.6 0.7 copy-start.1

commit v2 on v1

v2 whole, which is shorter than its diff:
```python
import math

import jax
import jax.numpy as jnp
import numpy as np
from jax import lax
from jax.experimental import pallas as pl
from jax.experimental.pallas import tpu as pltpu
from jax.sharding import PartitionSpec as P

D = 128
TILE = 128
REACH = 2
HALO = 256
BLOCKS = 32
EXT = 40
NODE = BLOCKS * TILE
SLOTS = 640
FR_DEV = 128
OFFSETS = tuple(o for o in range(-REACH, REACH + 1) if o != 0)
LOG2E = math.log2(math.e)
CENTRE = 6.0
GROUP = 2
UNROLL = 8
NONE = -1e30

f32, bf16, i32 = jnp.float32, jnp.bfloat16, jnp.int32
MESH = pl.DeviceIdType.MESH


def split3(x):
    high = x.astype(bf16).astype(f32)
    rest = x - high
    mid = rest.astype(bf16).astype(f32)
    return high, mid, rest - mid


def feature_maps():
    recv = np.zeros((128, 32), np.float32)
    send = np.zeros((32, 16), np.float32)
    pairs = ((0, 0), (0, 1), (1, 0), (1, 1), (0, 2), (2, 0))
    for p, (a, b) in enumerate(pairs):
        for c in range(3):
            recv[3 * a + c, 3 * p + c] = -2.0
            send[3 * p + c, 3 * b + c] = 1.0
    for c in range(3):
        recv[13 + c, 18 + c] = 1.0
        send[18 + c, 12] = 1.0
        recv[12, 21 + c] = 1.0
        send[21 + c, 13 + c] = 1.0
    return jnp.asarray(recv, bf16), jnp.asarray(send, bf16)


def aux_columns(rows):
    cols = jnp.transpose(jnp.concatenate([rows, rows], axis=0))
    return jnp.concatenate([cols, jnp.zeros((cols.shape[0], 96), f32)], axis=1)


def halo_kernel(lat_h, pos_h, mass_h, wv_h, tb_h, tc, sr_h, fa_h, fb_h,
                ws_h, wmsg_h, woff_h, bias_h, wo_h, gain_h, ids_h,
                A, B, V, lm, codes, lmult, acc, lat, w_in, wc2, rows_out, want,
                pos, mass, wv, tb, sr, fa, fb, w_offset, w_out, ids,
                rows_s, hot, sval, saux, rval, raux, isem, ssem, rsem):
    s = lax.axis_index("space")
    f = lax.axis_index("frag")
    n_space = lax.axis_size("space")
    loads = [pltpu.make_async_copy(src, dst, isem.at[i]) for i, (src, dst) in enumerate((
        (pos_h, pos), (mass_h, mass), (lat_h, lat), (wv_h, wv), (sr_h, sr), (tb_h, tb), (fa_h, fa), (fb_h, fb),
        (ws_h, w_in.at[0:128]), (wmsg_h, w_in.at[128:256]), (woff_h, w_offset), (wo_h, w_out),
        (bias_h, rows_out.at[0:1]), (gain_h, rows_out.at[1:2]), (ids_h, ids)))]
    for c in loads:
        c.start()
    barrier = pltpu.get_barrier_semaphore()
    for o in OFFSETS:
        @pl.when((s + o >= 0) & (s + o < n_space))
        def _():
            pl.semaphore_signal(barrier, inc=1, device_id=(s + o, f), device_id_type=MESH)

    loads[0].wait()
    loads[1].wait()
    x = (pos[...] - CENTRE) * LOG2E
    xh, xm, xl = split3(x)
    mh, mm, ml = split3(mass[...])
    sq = x * x
    norm = sq[0:1] + sq[1:2] + sq[2:3]
    nh, nm, nl = split3(norm)
    rows_s[...] = jnp.concatenate([xh, xm, xl, mh, mm, ml, jnp.ones((1, NODE), f32), nh, nm, nl], axis=0)
    for b in range(BLOCKS):
        V[b, :, 128:256] = aux_columns(rows_s[:, b * TILE:(b + 1) * TILE]).astype(bf16)
    loads[2].wait()
    loads[3].wait()
    loads[4].wait()
    values = jnp.dot(lat[...], wv[...], preferred_element_type=f32).astype(bf16)
    V[0:BLOCKS, :, 0:128] = values.reshape(BLOCKS, TILE, D)

    def copies(k):
        o = OFFSETS[k]
        dev = (s + o, f)
        return (
            pltpu.make_async_remote_copy(
                src_ref=sval.at[k], dst_ref=rval.at[k], send_sem=ssem.at[0, k], recv_sem=rsem.at[0, k],
                device_id=dev, device_id_type=MESH),
            pltpu.make_async_remote_copy(
                src_ref=saux.at[k], dst_ref=raux.at[k], send_sem=ssem.at[1, k], recv_sem=rsem.at[1, k],
                device_id=dev, device_id_type=MESH),
        )

    idx = sr[...].astype(f32)
    idx = jnp.transpose(jnp.concatenate([idx, idx], axis=0))
    lane = lax.broadcasted_iota(i32, (HALO, TILE), 1).astype(f32)
    for first, pair in ((True, (0, 3)), (False, (1, 2))):
        for p, k in enumerate(pair):
            col = idx[:, k:k + 1]
            high = jnp.floor(col * (1.0 / TILE))
            low = col - high * TILE
            code = jnp.where(low == lane, high, -1.0).astype(bf16)
            for b in range(BLOCKS):
                hot[p * HALO:(p + 1) * HALO, b * TILE:(b + 1) * TILE] = jnp.where(
                    code == jnp.asarray(b, bf16), 1.0, 0.0).astype(bf16)
        got = jnp.dot(hot[...], V[0:BLOCKS].reshape(NODE, 256), preferred_element_type=f32)
        if first:
            pl.semaphore_wait(barrier, jnp.minimum(s, REACH) + jnp.minimum(n_space - 1 - s, REACH))
        for p, k in enumerate(pair):
            part = got[p * HALO:(p + 1) * HALO]
            sval[k] = part[:, 0:128].astype(bf16)
            saux[k] = jnp.transpose(part[:, 128:256])[0:16].astype(bf16)
            o = OFFSETS[k]

            @pl.when((s + o >= 0) & (s + o < n_space))
            def _():
                for c in copies(k):
                    c.start()

            @pl.when((s - o < 0) | (s - o >= n_space))
            def _():
                rval[k] = jnp.zeros((HALO, D), bf16)
                raux[k] = jnp.zeros((16, HALO), bf16)

    for c in loads[5:]:
        c.wait()
    slot = lax.broadcasted_iota(i32, (BLOCKS, SLOTS), 1)
    rhot = (lax.broadcasted_iota(i32, (BLOCKS, SLOTS), 0) == tb[0:1, :]) & (slot < tc[0])
    chot = lax.broadcasted_iota(i32, (128, SLOTS), 0) == tb[1:2, :]
    count = lax.dot_general(
        jnp.where(rhot, 1.0, 0.0).astype(bf16), jnp.where(chot, 1.0, 0.0).astype(bf16),
        (((1,), (1,)), ((), ())), preferred_element_type=f32)
    live = jnp.where(count > 0.0, 1.0, 0.0)
    before = lax.broadcasted_iota(i32, (128, 128), 0) < lax.broadcasted_iota(i32, (128, 128), 1)
    place = jnp.dot(live.astype(bf16), jnp.where(before, 1.0, 0.0).astype(bf16), preferred_element_type=f32)
    place = jnp.where(count > 0.0, place, -1.0)
    col_id = lax.broadcasted_iota(i32, (BLOCKS, 128), 1).astype(f32)
    packed = col_id + 64.0 * count
    listed = jnp.zeros((BLOCKS, 128), f32)
    for c in range(EXT):
        listed = listed + jnp.where(place[:, c:c + 1] == col_id, packed[:, c:c + 1], 0.0)
    times = jnp.floor(listed * (1.0 / 64.0))
    sender = listed - 64.0 * times
    groups = jnp.maximum(jnp.floor((jnp.sum(live, axis=1, keepdims=True) + (GROUP - 1)) * (1.0 / GROUP)), 1.0)
    codes[...] = jnp.where(col_id == 127.0, groups, sender).astype(i32)
    lmult[...] = jnp.where(times > 0.0, jnp.log2(jnp.maximum(times, 1.0)), NONE)

    A[...] = jnp.dot(V[0:BLOCKS, :, 128:256].reshape(NODE, 128), fa[...],
                     preferred_element_type=f32).astype(bf16).reshape(BLOCKS, TILE, 32)
    own_b = jnp.dot(fb[...], rows_s[...].astype(bf16), preferred_element_type=f32).astype(bf16)
    lmass = jnp.log2(mass[...])
    for b in range(BLOCKS):
        B[b] = own_b[:, b * TILE:(b + 1) * TILE]
        lm[b] = lmass[:, b * TILE:(b + 1) * TILE]

    fid = ids[...].astype(f32)
    high = jnp.floor(fid * (1.0 / FR_DEV))
    want[0:1] = high
    want[1:2] = fid - high * FR_DEV
    woff = w_offset[...] * (1.0 / LOG2E)
    wh = woff.astype(bf16).astype(f32)
    wm = woff - wh
    w_in[256:384] = jnp.concatenate(
        [wh, wh, wh, jnp.zeros((7, 128), f32), wm, wm, wm, jnp.zeros((103, 128), f32)], axis=0).astype(bf16)
    w_in[384:512] = jnp.concatenate([wh, wh, wh, jnp.zeros((119, 128), f32)], axis=0).astype(bf16)
    wo = w_out[...].astype(f32)
    wc = wo - jnp.mean(wo, axis=1, keepdims=True)
    wc_h = wc.astype(bf16)
    wc2[0:128] = wc_h
    wc2[128:256] = (wc - wc_h.astype(f32)).astype(bf16)

    row_id = lax.broadcasted_iota(i32, (128, 128), 0)
    mass_map = jnp.where((row_id >= 9) & (row_id < 12), 1.0, 0.0).astype(bf16)
    for b in range(BLOCKS):
        own = V[b, :, 128:256]
        acc[b, :, 0:128] = jnp.zeros((TILE, 128), f32)
        acc[b, :, 128:256] = jnp.dot(own, mass_map, preferred_element_type=f32) * own.astype(f32)

    for k in (0, 3, 1, 2):
        o = OFFSETS[k]

        @pl.when((s - o >= 0) & (s - o < n_space))
        def _():
            for c in copies(k):
                c.wait_recv()

        aux = raux[k].astype(f32)
        V[BLOCKS + 2 * k:BLOCKS + 2 * k + 2, :, 0:128] = rval[k].reshape(2, TILE, D)
        V[BLOCKS + 2 * k:BLOCKS + 2 * k + 2, :, 128:256] = aux_columns(aux).astype(bf16).reshape(2, TILE, 128)
        far_b = jnp.dot(fb[...], raux[k], preferred_element_type=f32).astype(bf16)
        far_mass = aux[9:10] + aux[10:11] + aux[11:12]
        far_lm = jnp.where(far_mass > 0.0, jnp.log2(jnp.maximum(far_mass, 1e-30)), NONE)
        for h in range(2):
            B[BLOCKS + 2 * k + h] = far_b[:, h * TILE:(h + 1) * TILE]
            lm[BLOCKS + 2 * k + h] = far_lm[:, h * TILE:(h + 1) * TILE]

    for k in range(4):
        o = OFFSETS[k]

        @pl.when((s + o >= 0) & (s + o < n_space))
        def _():
            for c in copies(k):
                c.wait_send()


def tile_kernel(codes, lmult, A, B, V, lm, acc_in, lat, w_in, wc2, rows, acc, upd_h, upd, wb, osem):
    wb[...] = jnp.zeros_like(wb)
    total = lax.fori_loop(0, BLOCKS, lambda r, t: t + codes[r, 127], 0)

    def advance(state):
        out = []
        for _ in range(UNROLL):
            r, g = state
            over = g + 1 >= codes[r, 127]
            state = (jnp.minimum(jnp.where(over, r + 1, r), BLOCKS - 1), jnp.where(over, 0, g + 1))
            out.append(state)
        return out

    def step(it, states):
        now, last = states[:UNROLL], states[UNROLL:]
        for q in range(UNROLL):
            r, g = last[q]
            sent = jnp.concatenate([V[codes[r, g * GROUP + u]] for u in range(GROUP)], axis=0)
            acc[r] = acc[r] + jnp.dot(wb[q], sent, preferred_element_type=f32)
            r, g = now[q]
            off = jnp.where(it * UNROLL + q < total, 0.0, NONE).astype(f32)
            senders = [codes[r, g * GROUP + u] for u in range(GROUP)]
            sq = jnp.dot(A[r], jnp.concatenate([B[c] for c in senders], axis=1), preferred_element_type=f32)
            for u in range(GROUP):
                level = lm[senders[u]] + (lmult[r, g * GROUP + u] + off)
                d2 = jnp.maximum(sq[:, u * TILE:(u + 1) * TILE], 1e-12)
                wb[q, :, u * TILE:(u + 1) * TILE] = jnp.exp2(level - d2 * lax.rsqrt(d2)).astype(bf16)
        return tuple(advance(now[-1])) + tuple(now)

    zero = jnp.int32(0)
    first = [(zero, zero)] + advance((zero, zero))[:UNROLL - 1]
    lax.fori_loop(0, (total + UNROLL - 1) // UNROLL + 1, step, tuple(first) + ((zero, zero),) * UNROLL)

    bias_row = rows[0:1]
    gain_row = rows[1:2]
    PIECES = 8
    outs = [pltpu.make_async_copy(upd.at[pl.ds(i * (NODE // PIECES), NODE // PIECES)],
                                  upd_h.at[pl.ds(i * (NODE // PIECES), NODE // PIECES)], osem.at[i])
            for i in range(PIECES)]

    def stage1(b):
        tot = acc[b, :, 128:256]
        rs = lax.rsqrt(tot[:, 12:13])
        agg = (acc[b, :, 0:128] * rs).astype(bf16)
        q = tot * (rs * rs) - V[b, :, 128:256].astype(f32)
        qh = q.astype(bf16)
        qm = (q - qh.astype(f32)).astype(bf16)
        return jnp.concatenate([lat[b * TILE:(b + 1) * TILE], agg, qh, qm], axis=1)

    def stage2(cat):
        pre = jnp.dot(cat, w_in[...], preferred_element_type=f32) + bias_row
        hid = (pre * (0.5 + 0.5 * jnp.tanh(0.5 * pre))).astype(bf16)
        return jnp.concatenate([hid, hid], axis=1)

    def stage3(b, hid):
        cen = jnp.dot(hid, wc2[...], preferred_element_type=f32)
        var = jnp.mean(cen * cen, axis=1, keepdims=True)
        out = lat[b * TILE:(b + 1) * TILE].astype(f32) + cen * lax.rsqrt(var + 1e-5) * gain_row
        upd[b * TILE:(b + 1) * TILE] = out.astype(bf16)

    cats, hids = {}, {}
    for b in range(BLOCKS + 2):
        if b >= 2:
            stage3(b - 2, hids.pop(b - 2))
            if (b - 1) % (BLOCKS // PIECES) == 0:
                outs[(b - 2) // (BLOCKS // PIECES)].start()
        if 1 <= b <= BLOCKS:
            hids[b - 1] = stage2(cats.pop(b - 1))
        if b < BLOCKS:
            cats[b] = stage1(b)
    for c in outs:
        c.wait()


NZ = 8
NY = 4


def pool_kernel(upd, want, out, hot, part, g1, a2, g2, a3, g3, full, s1, r1, s2, r2, s3, r3, s4, r4):
    s = lax.axis_index("space")
    f = lax.axis_index("frag")
    nf = lax.axis_size("frag")
    y = s // NZ
    z = lax.rem(s, NZ)
    barrier = pltpu.get_barrier_semaphore()

    def dev(dy, dz, df):
        return (lax.rem(y + dy, NY) * NZ + lax.rem(z + dz, NZ), lax.rem(f + df, nf))

    peers = [dev(0, 0, i) for i in range(1, nf)] + [dev(i, 0, 0) for i in range(1, NY)]
    peers += [dev(0, i, 0) for i in range(1, NZ)]
    for p in peers:
        pl.semaphore_signal(barrier, inc=1, device_id=p, device_id_type=MESH)

    def remote(src, dst, send, recv, i, to):
        return pltpu.make_async_remote_copy(
            src_ref=src, dst_ref=dst, send_sem=send.at[i - 1], recv_sem=recv.at[i - 1],
            device_id=to, device_id_type=MESH)

    c1 = {i: remote(part.at[i], g1.at[i - 1], s1, r1, i, dev(0, 0, i)) for i in range(1, nf)}
    c2 = {i: remote(a2.at[lax.rem(y + i, NY)], g2.at[i - 1], s2, r2, i, dev(i, 0, 0)) for i in range(1, NY)}
    c3 = {i: remote(a3, g3.at[i - 1], s3, r3, i, dev(0, i, 0)) for i in range(1, NZ)}
    c4 = {i: remote(full.at[y], full.at[y], s4, r4, i, dev(i, 0, 0)) for i in range(1, NY)}

    sub = lax.broadcasted_iota(i32, (FR_DEV, TILE), 0).astype(f32).astype(bf16)
    high = want[0:1]
    low = want[1:2]

    def build(slot, i):
        t = lax.rem(f + i, nf).astype(f32)
        row = jnp.where(high == t, low, -1.0).astype(bf16)
        for b in range(BLOCKS):
            cut = jnp.broadcast_to(row[:, b * TILE:(b + 1) * TILE], (FR_DEV, TILE))
            hot[slot, :, b * TILE:(b + 1) * TILE] = jnp.where(cut == sub, 1.0, 0.0).astype(bf16)

    order = (4, 3, 5, 2, 6, 1, 7, 0)
    build(0, order[0])
    for n, i in enumerate(order):
        if n + 1 < nf:
            build((n + 1) % 2, order[n + 1])
        sums = jnp.dot(hot[n % 2], upd[...], preferred_element_type=f32)
        if n == 0:
            pl.semaphore_wait(barrier, nf + NY + NZ - 3)
        if i:
            part[i] = sums.astype(bf16)
            c1[i].start()
        else:
            total = sums
    for i in order[:-1]:
        c1[i].wait_recv()
        total = total + g1[i - 1].astype(f32)
    a2[...] = total.astype(bf16).reshape(NY, FR_DEV // NY, D)
    for i in (2, 1, 3):
        c2[i].start()
    total = a2[y].astype(f32)
    for i in (1, 3, 2):
        c2[i].wait_recv()
        total = total + g2[i - 1].astype(f32)
    a3[...] = total.astype(bf16)
    for i in (4, 3, 5, 2, 6, 1, 7):
        c3[i].start()
    total = a3[...].astype(f32)
    for i in (1, 7, 2, 6, 3, 5, 4):
        c3[i].wait_recv()
        total = total + g3[i - 1].astype(f32)
    full[y] = total
    for i in (2, 1, 3):
        c4[i].start()
    for i in (1, 3, 2):
        c4[i].wait_recv()
    out[...] = full[...].reshape(FR_DEV, D)
    for group in (c1, c2, c3, c4):
        for c in group.values():
            c.wait_send()


def shards(latents, positions, masses, w_value, w_self, w_message, w_offset, bias_hidden, w_out, norm_gain,
           tile_blocks, tile_count, send_rows, frag_ids):
    ns, nf = lax.axis_size("space"), lax.axis_size("frag")
    vm = pl.BlockSpec(memory_space=pltpu.VMEM)
    sm = pl.BlockSpec(memory_space=pltpu.SMEM)
    hbm = pl.BlockSpec(memory_space=pltpu.HBM)
    fa, fb = feature_maps()
    dma = pltpu.SemaphoreType.DMA
    vmem = pltpu.VMEM
    limit = 36 << 20
    pin = lambda a: pltpu.with_memory_space_constraint(a, pltpu.HBM)
    A, B, V, lm, codes, lmult, acc, lat, w_in, wc2, rows, want = pl.pallas_call(
        halo_kernel,
        out_shape=(
            jax.ShapeDtypeStruct((BLOCKS, TILE, 32), bf16),
            jax.ShapeDtypeStruct((EXT, 32, TILE), bf16),
            jax.ShapeDtypeStruct((EXT, TILE, 256), bf16),
            jax.ShapeDtypeStruct((EXT, 1, TILE), f32),
            jax.ShapeDtypeStruct((BLOCKS, 128), i32),
            jax.ShapeDtypeStruct((BLOCKS, 128), f32),
            jax.ShapeDtypeStruct((BLOCKS, TILE, 256), f32),
            jax.ShapeDtypeStruct((NODE, D), bf16),
            jax.ShapeDtypeStruct((512, D), bf16),
            jax.ShapeDtypeStruct((256, D), bf16),
            jax.ShapeDtypeStruct((2, D), f32),
            jax.ShapeDtypeStruct((2, NODE), f32),
        ),
        in_specs=[hbm] * 5 + [sm] + [hbm] * 10,
        out_specs=(vm,) * 12,
        scratch_shapes=[
            vmem((3, NODE), f32), vmem((1, NODE), f32), vmem((D, D), bf16),
            vmem((2, SLOTS), i32), vmem((4, HALO), i32), vmem((128, 32), bf16), vmem((32, 16), bf16),
            vmem((3, D), f32), vmem((D, D), bf16), vmem((1, NODE), i32),
            vmem((16, NODE), f32),
            vmem((2 * HALO, NODE), bf16),
            vmem((4, HALO, D), bf16),
            vmem((4, 16, HALO), bf16),
            vmem((4, HALO, D), bf16),
            vmem((4, 16, HALO), bf16),
            dma((15,)),
            dma((2, 4)),
            dma((2, 4)),
        ],
        compiler_params=pltpu.CompilerParams(collective_id=0, has_side_effects=True, vmem_limit_bytes=limit),
    )(pin(latents), pin(positions), pin(masses.reshape(1, NODE)), pin(w_value), pin(tile_blocks), tile_count,
      pin(send_rows), pin(fa), pin(fb),
      pin(w_self), pin(w_message), pin(w_offset), pin(bias_hidden.reshape(1, D)), pin(w_out),
      pin(norm_gain.reshape(1, D)),
      pin(frag_ids.reshape(1, NODE)))

    _, updated, upd = pl.pallas_call(
        tile_kernel,
        out_shape=(
            jax.ShapeDtypeStruct((BLOCKS, TILE, 256), f32),
            jax.ShapeDtypeStruct((NODE, D), bf16),
            jax.ShapeDtypeStruct((NODE, D), bf16),
        ),
        in_specs=[sm, sm] + [vm] * 9,
        out_specs=(vm, hbm, vm),
        input_output_aliases={6: 0},
        scratch_shapes=[vmem((UNROLL, TILE, GROUP * TILE), bf16), dma((8,))],
        compiler_params=pltpu.CompilerParams(vmem_limit_bytes=limit),
    )(codes, lmult, A, B, V, lm, acc, lat, w_in, wc2, rows)

    pooled = pl.pallas_call(
        pool_kernel,
        out_shape=jax.ShapeDtypeStruct((FR_DEV, D), f32),
        in_specs=[vm, vm],
        out_specs=vm,
        scratch_shapes=[
            vmem((2, FR_DEV, NODE), bf16),
            vmem((nf, FR_DEV, D), bf16),
            vmem((nf - 1, FR_DEV, D), bf16),
            vmem((NY, FR_DEV // NY, D), bf16),
            vmem((NY - 1, FR_DEV // NY, D), bf16),
            vmem((FR_DEV // NY, D), bf16),
            vmem((NZ - 1, FR_DEV // NY, D), bf16),
            vmem((NY, FR_DEV // NY, D), f32),
            dma((nf - 1,)), dma((nf - 1,)),
            dma((NY - 1,)), dma((NY - 1,)),
            dma((NZ - 1,)), dma((NZ - 1,)),
            dma((NY - 1,)), dma((NY - 1,)),
        ],
        compiler_params=pltpu.CompilerParams(collective_id=1, has_side_effects=True, vmem_limit_bytes=limit),
    )(upd, want)
    return updated, pooled * math.sqrt(FR_DEV * nf / (NODE * ns * nf))


def solution(mesh):
    own = P(("space", "frag"))
    return jax.shard_map(
        shards,
        mesh=mesh,
        in_specs=(
            P(("space", "frag"), None), P(None, ("space", "frag")), own,
            P(), P(), P(), P(), P(), P(), P(),
            P(None, ("space", "frag")), own, P(None, ("space", "frag")), own,
        ),
        out_specs=(P(("space", "frag"), None), P("frag", None)),
        check_vma=False,
    )
```

time: 87.2 us -> 67.3 us (0.77)
  the two profiles are of different devices: /device:TPU:1 before, /device:TPU:2 now
where the time goes in v2:
time: 67.3 us; the launch traced here: 66.3 us
  Pallas kernels  64.3 us (96%)
  between operations  1.31 us (2%)
    pallas_call x1, Pallas kernels, shards(): pl.pallas_call(pool_kernel, out_shape=jax.ShapeDtypeStruct((FR_DEV, D), f...  33.6 us
    pallas_call x1, Pallas kernels, shards(): pl.pallas_call(tile_kernel, out_shape=(jax.ShapeDtypeStruct((BLOCKS, TILE...  17.1 us
    pallas_call x1, Pallas kernels, shards(): pl.pallas_call(halo_kernel, out_shape=(jax.ShapeDtypeStruct((BLOCKS, TILE...  13.6 us

profile of v2, /device:TPU:2, one launch (start us, length us, event | category | flops | bytes accessed | tf_op | source)
XLA Modules:
  0.0 66.3 jit_solution(17516544251976722157)
XLA Ops:
  1.3 13.6 %shard_map.167 = (bf16[32,128,32]{2,1,0:T(8,128)(2,1)S(1)}, bf16[40,32,128]{2,1,0:T(8,128)(2,1)S(1)}, bf16[40,128,256]{2,1,0:T(8,128)(2,1)S(1)}, f32[40,1,128]{2...) custom-call(bf16[4096,128]{1,0:T(8,128)(2,1)} %lat_h.1, ...), custom_call_target="tpu_custom_call" | custom-call | tf_op jit(solution)/shard_map/pallas_call | solution.py:387
  14.8 17.1 %shard_map.168 = (f32[32,128,256]{2,1,0:T(8,128)S(1)}, bf16[4096,128]{1,0:T(8,128)(2,1)}, bf16[4096,128]{1,0:T(8,128)(2,1)S(1)}) custom-call(s32[32,128]{1,0:T(8,128)S(1)} %get-tuple-element.16.codes, f32[32,128]{1,0:T(8,128)S(1)} %get-tuple-element.17.lmult, bf16[32,128,32]{2,1,0:T(8,128)(2,1)S(1)} %get-tuple-element.18.A, ...), custom_call_target="tpu_custom_call", output_to_operand_aliasing={{0}: (6, {})} | custom-call | tf_op jit(solution)/shard_map/pallas_call | solution.py:426
  32.0 33.6 %shard_map.169 = f32[128,128]{1,0:T(8,128)S(1)} custom-call(bf16[4096,128]{1,0:T(8,128)(2,1)S(1)} %get-tuple-element.28.upd, f32[2,4096]{1,0:T(2,128)S(1)} %get-tuple-element.29.want), custom_call_target="tpu_custom_call" | custom-call | tf_op jit(solution)/shard_map/pallas_call | solution.py:440
  65.6 0.6 broadcast_multiply_fusion

commit v3 on v2

--- a/solution.py
+++ b/solution.py
@@ -21,7 +21,7 @@
 LOG2E = math.log2(math.e)
 CENTRE = 6.0
 GROUP = 2
-UNROLL = 8
+UNROLL = 16
 NONE = -1e30
 
 f32, bf16, i32 = jnp.float32, jnp.bfloat16, jnp.int32
@@ -65,7 +65,7 @@
     f = lax.axis_index("frag")
     n_space = lax.axis_size("space")
     loads = [pltpu.make_async_copy(src, dst, isem.at[i]) for i, (src, dst) in enumerate((
-        (pos_h, pos), (mass_h, mass), (lat_h, lat), (wv_h, wv), (sr_h, sr), (tb_h, tb), (fa_h, fa), (fb_h, fb),
+        (sr_h, sr), (pos_h, pos), (mass_h, mass), (lat_h, lat), (wv_h, wv), (tb_h, tb), (fa_h, fa), (fb_h, fb),
         (ws_h, w_in.at[0:128]), (wmsg_h, w_in.at[128:256]), (woff_h, w_offset), (wo_h, w_out),
         (bias_h, rows_out.at[0:1]), (gain_h, rows_out.at[1:2]), (ids_h, ids)))]
     for c in loads:
@@ -76,8 +76,8 @@
         def _():
             pl.semaphore_signal(barrier, inc=1, device_id=(s + o, f), device_id_type=MESH)
 
-    loads[0].wait()
     loads[1].wait()
+    loads[2].wait()
     x = (pos[...] - CENTRE) * LOG2E
     xh, xm, xl = split3(x)
     mh, mm, ml = split3(mass[...])
@@ -87,9 +87,9 @@
     rows_s[...] = jnp.concatenate([xh, xm, xl, mh, mm, ml, jnp.ones((1, NODE), f32), nh, nm, nl], axis=0)
     for b in range(BLOCKS):
         V[b, :, 128:256] = aux_columns(rows_s[:, b * TILE:(b + 1) * TILE]).astype(bf16)
-    loads[2].wait()
     loads[3].wait()
     loads[4].wait()
+    loads[0].wait()
     values = jnp.dot(lat[...], wv[...], preferred_element_type=f32).astype(bf16)
     V[0:BLOCKS, :, 0:128] = values.reshape(BLOCKS, TILE, D)
 
@@ -190,23 +190,29 @@
         acc[b, :, 0:128] = jnp.zeros((TILE, 128), f32)
         acc[b, :, 128:256] = jnp.dot(own, mass_map, preferred_element_type=f32) * own.astype(f32)
 
-    for k in (0, 3, 1, 2):
-        o = OFFSETS[k]
-
-        @pl.when((s - o >= 0) & (s - o < n_space))
-        def _():
-            for c in copies(k):
-                c.wait_recv()
-
-        aux = raux[k].astype(f32)
-        V[BLOCKS + 2 * k:BLOCKS + 2 * k + 2, :, 0:128] = rval[k].reshape(2, TILE, D)
-        V[BLOCKS + 2 * k:BLOCKS + 2 * k + 2, :, 128:256] = aux_columns(aux).astype(bf16).reshape(2, TILE, 128)
-        far_b = jnp.dot(fb[...], raux[k], preferred_element_type=f32).astype(bf16)
+    for pair in ((0, 3), (1, 2)):
+        for k in pair:
+            o = OFFSETS[k]
+
+            @pl.when((s - o >= 0) & (s - o < n_space))
+            def _():
+                for c in copies(k):
+                    c.wait_recv()
+
+        aux = jnp.concatenate([raux[k] for k in pair], axis=1)
+        far_b = jnp.dot(fb[...], aux, preferred_element_type=f32).astype(bf16)
+        aux = aux.astype(f32)
+        cols = aux_columns(aux).astype(bf16)
         far_mass = aux[9:10] + aux[10:11] + aux[11:12]
         far_lm = jnp.where(far_mass > 0.0, jnp.log2(jnp.maximum(far_mass, 1e-30)), NONE)
-        for h in range(2):
-            B[BLOCKS + 2 * k + h] = far_b[:, h * TILE:(h + 1) * TILE]
-            lm[BLOCKS + 2 * k + h] = far_lm[:, h * TILE:(h + 1) * TILE]
+        for p, k in enumerate(pair):
+            first = BLOCKS + 2 * k
+            V[first:first + 2, :, 0:128] = rval[k].reshape(2, TILE, D)
+            V[first:first + 2, :, 128:256] = cols[p * HALO:(p + 1) * HALO].reshape(2, TILE, 128)
+            for h in range(2):
+                at = p * HALO + h * TILE
+                B[first + h] = far_b[:, at:at + TILE]
+                lm[first + h] = far_lm[:, at:at + TILE]
 
     for k in range(4):
         o = OFFSETS[k]
@@ -232,16 +238,23 @@
 
     def step(it, states):
         now, last = states[:UNROLL], states[UNROLL:]
+        def distances(q):
+            r, g = now[q]
+            pair = jnp.concatenate([B[codes[r, g * GROUP + u]] for u in range(GROUP)], axis=1)
+            return jnp.dot(A[r], pair, preferred_element_type=f32)
+
+        ahead = distances(0)
         for q in range(UNROLL):
             r, g = last[q]
             sent = jnp.concatenate([V[codes[r, g * GROUP + u]] for u in range(GROUP)], axis=0)
             acc[r] = acc[r] + jnp.dot(wb[q], sent, preferred_element_type=f32)
+            sq = ahead
+            if q + 1 < UNROLL:
+                ahead = distances(q + 1)
             r, g = now[q]
             off = jnp.where(it * UNROLL + q < total, 0.0, NONE).astype(f32)
-            senders = [codes[r, g * GROUP + u] for u in range(GROUP)]
-            sq = jnp.dot(A[r], jnp.concatenate([B[c] for c in senders], axis=1), preferred_element_type=f32)
             for u in range(GROUP):
-                level = lm[senders[u]] + (lmult[r, g * GROUP + u] + off)
+                level = lm[codes[r, g * GROUP + u]] + (lmult[r, g * GROUP + u] + off)
                 d2 = jnp.maximum(sq[:, u * TILE:(u + 1) * TILE], 1e-12)
                 wb[q, :, u * TILE:(u + 1) * TILE] = jnp.exp2(level - d2 * lax.rsqrt(d2)).astype(bf16)
         return tuple(advance(now[-1])) + tuple(now)
@@ -325,26 +338,33 @@
     high = want[0:1]
     low = want[1:2]
 
-    def build(slot, i):
+    def build(slot, place, i):
         t = lax.rem(f + i, nf).astype(f32)
         row = jnp.where(high == t, low, -1.0).astype(bf16)
         for b in range(BLOCKS):
             cut = jnp.broadcast_to(row[:, b * TILE:(b + 1) * TILE], (FR_DEV, TILE))
-            hot[slot, :, b * TILE:(b + 1) * TILE] = jnp.where(cut == sub, 1.0, 0.0).astype(bf16)
+            hot[slot, place * FR_DEV:(place + 1) * FR_DEV, b * TILE:(b + 1) * TILE] = jnp.where(
+                cut == sub, 1.0, 0.0).astype(bf16)
 
     order = (4, 3, 5, 2, 6, 1, 7, 0)
-    build(0, order[0])
-    for n, i in enumerate(order):
-        if n + 1 < nf:
-            build((n + 1) % 2, order[n + 1])
-        sums = jnp.dot(hot[n % 2], upd[...], preferred_element_type=f32)
-        if n == 0:
+    BATCH = 4
+    for n in range(BATCH):
+        build(0, n, order[n])
+    for slot in range(nf // BATCH):
+        if slot + 1 < nf // BATCH:
+            for n in range(BATCH):
+                build(slot + 1, n, order[(slot + 1) * BATCH + n])
+        sums = jnp.dot(hot[slot], upd[...], preferred_element_type=f32)
+        if slot == 0:
             pl.semaphore_wait(barrier, nf + NY + NZ - 3)
-        if i:
-            part[i] = sums.astype(bf16)
-            c1[i].start()
-        else:
-            total = sums
+        for n in range(BATCH):
+            i = order[slot * BATCH + n]
+            mine = sums[n * FR_DEV:(n + 1) * FR_DEV]
+            if i:
+                part[i] = mine.astype(bf16)
+                c1[i].start()
+            else:
+                total = mine
     for i in order[:-1]:
         c1[i].wait_recv()
         total = total + g1[i - 1].astype(f32)
@@ -443,7 +463,7 @@
         in_specs=[vm, vm],
         out_specs=vm,
         scratch_shapes=[
-            vmem((2, FR_DEV, NODE), bf16),
+            vmem((2, 4 * FR_DEV, NODE), bf16),
             vmem((nf, FR_DEV, D), bf16),
             vmem((nf - 1, FR_DEV, D), bf16),
             vmem((NY, FR_DEV // NY, D), bf16),

time: 67.3 us -> 65 us (0.966)
  Pallas kernels: 64.3 us -> 62.7 us
    pallas_call x1, Pallas kernels: 17.1 us -> 13.7 us  [shards(): pl.pallas_call(tile_kernel, out_shape=(jax.ShapeDtypeStruct((BLOCKS, TILE...]
    pallas_call x1, Pallas kernels: 33.6 us -> 35.5 us  [shards(): pl.pallas_call(pool_kernel, out_shape=jax.ShapeDtypeStruct((FR_DEV, D), f...]
where the time goes in v3:
time: 65 us; the launch traced here: 64.6 us
  Pallas kernels  62.7 us (96%)
  between operations  1.31 us (2%)
    pallas_call x1, Pallas kernels, shards(): pl.pallas_call(pool_kernel, out_shape=jax.ShapeDtypeStruct((FR_DEV, D), f...  35.5 us
    pallas_call x1, Pallas kernels, shards(): pl.pallas_call(tile_kernel, out_shape=(jax.ShapeDtypeStruct((BLOCKS, TILE...  13.7 us
    pallas_call x1, Pallas kernels, shards(): pl.pallas_call(halo_kernel, out_shape=(jax.ShapeDtypeStruct((BLOCKS, TILE...  13.5 us

profile of v3, /device:TPU:2, one launch (start us, length us, event | category | flops | bytes accessed | tf_op | source)
XLA Modules:
  0.0 64.6 jit_solution(13897030873109034752)
XLA Ops:
  1.3 13.5 %shard_map.167 = (bf16[32,128,32]{2,1,0:T(8,128)(2,1)S(1)}, bf16[40,32,128]{2,1,0:T(8,128)(2,1)S(1)}, bf16[40,128,256]{2,1,0:T(8,128)(2,1)S(1)}, f32[40,1,128]{2...) custom-call(bf16[4096,128]{1,0:T(8,128)(2,1)} %lat_h.1, ...), custom_call_target="tpu_custom_call" | custom-call | tf_op jit(solution)/shard_map/pallas_call | solution.py:407
  14.7 13.7 %shard_map.168 = (f32[32,128,256]{2,1,0:T(8,128)S(1)}, bf16[4096,128]{1,0:T(8,128)(2,1)}, bf16[4096,128]{1,0:T(8,128)(2,1)S(1)}) custom-call(s32[32,128]{1,0:T(8,128)S(1)} %get-tuple-element.16.codes, f32[32,128]{1,0:T(8,128)S(1)} %get-tuple-element.17.lmult, bf16[32,128,32]{2,1,0:T(8,128)(2,1)S(1)} %get-tuple-element.18.A, ...), custom_call_target="tpu_custom_call", output_to_operand_aliasing={{0}: (6, {})} | custom-call | tf_op jit(solution)/shard_map/pallas_call | solution.py:446
  28.5 35.5 %shard_map.169 = f32[128,128]{1,0:T(8,128)S(1)} custom-call(bf16[4096,128]{1,0:T(8,128)(2,1)S(1)} %get-tuple-element.28.upd, f32[2,4096]{1,0:T(2,128)S(1)} %get-tuple-element.29.want), custom_call_target="tpu_custom_call" | custom-call | tf_op jit(solution)/shard_map/pallas_call | solution.py:460
  64.0 0.6 broadcast_multiply_fusion

commit v4 on v3

--- a/solution.py
+++ b/solution.py
@@ -270,36 +270,44 @@
                                   upd_h.at[pl.ds(i * (NODE // PIECES), NODE // PIECES)], osem.at[i])
             for i in range(PIECES)]
 
-    def stage1(b):
-        tot = acc[b, :, 128:256]
+    STEP = 2
+    PARTS = BLOCKS // STEP
+
+    def rows_of(p):
+        return slice(p * STEP * TILE, (p + 1) * STEP * TILE)
+
+    def stage1(p):
+        got = acc[p * STEP:(p + 1) * STEP].reshape(STEP * TILE, 256)
+        tot = got[:, 128:256]
         rs = lax.rsqrt(tot[:, 12:13])
-        agg = (acc[b, :, 0:128] * rs).astype(bf16)
-        q = tot * (rs * rs) - V[b, :, 128:256].astype(f32)
+        agg = (got[:, 0:128] * rs).astype(bf16)
+        own = V[p * STEP:(p + 1) * STEP, :, 128:256].reshape(STEP * TILE, 128).astype(f32)
+        q = tot * (rs * rs) - own
         qh = q.astype(bf16)
         qm = (q - qh.astype(f32)).astype(bf16)
-        return jnp.concatenate([lat[b * TILE:(b + 1) * TILE], agg, qh, qm], axis=1)
+        return jnp.concatenate([lat[rows_of(p)], agg, qh, qm], axis=1)
 
     def stage2(cat):
         pre = jnp.dot(cat, w_in[...], preferred_element_type=f32) + bias_row
         hid = (pre * (0.5 + 0.5 * jnp.tanh(0.5 * pre))).astype(bf16)
         return jnp.concatenate([hid, hid], axis=1)
 
-    def stage3(b, hid):
+    def stage3(p, hid):
         cen = jnp.dot(hid, wc2[...], preferred_element_type=f32)
         var = jnp.mean(cen * cen, axis=1, keepdims=True)
-        out = lat[b * TILE:(b + 1) * TILE].astype(f32) + cen * lax.rsqrt(var + 1e-5) * gain_row
-        upd[b * TILE:(b + 1) * TILE] = out.astype(bf16)
+        out = lat[rows_of(p)].astype(f32) + cen * lax.rsqrt(var + 1e-5) * gain_row
+        upd[rows_of(p)] = out.astype(bf16)
 
     cats, hids = {}, {}
-    for b in range(BLOCKS + 2):
-        if b >= 2:
-            stage3(b - 2, hids.pop(b - 2))
-            if (b - 1) % (BLOCKS // PIECES) == 0:
-                outs[(b - 2) // (BLOCKS // PIECES)].start()
-        if 1 <= b <= BLOCKS:
-            hids[b - 1] = stage2(cats.pop(b - 1))
-        if b < BLOCKS:
-            cats[b] = stage1(b)
+    for p in range(PARTS + 2):
+        if p >= 2:
+            stage3(p - 2, hids.pop(p - 2))
+            if (p - 1) % (PARTS // PIECES) == 0:
+                outs[(p - 2) // (PARTS // PIECES)].start()
+        if 1 <= p <= PARTS:
+            hids[p - 1] = stage2(cats.pop(p - 1))
+        if p < PARTS:
+            cats[p] = stage1(p)
     for c in outs:
         c.wait()
 

time: 65 us -> 62.7 us (0.965); the launches traced: 64.6 us -> 63.1 us
  Pallas kernels: 62.7 us -> 61.1 us
    pallas_call x1, Pallas kernels: 13.7 us -> 10 us  [shards(): pl.pallas_call(tile_kernel, out_shape=(jax.ShapeDtypeStruct((BLOCKS, TILE...]
    pallas_call x1, Pallas kernels: 35.5 us -> 37.6 us  [shards(): pl.pallas_call(pool_kernel, out_shape=jax.ShapeDtypeStruct((FR_DEV, D), f...]
where the time goes in v4:
time: 62.7 us; the launch traced here: 63.1 us
  Pallas kernels  61.1 us (97%)
  between operations  1.31 us (2%)
  other arithmetic  0.64 us (1%)
    pallas_call x1, Pallas kernels, shards(): pl.pallas_call(pool_kernel, out_shape=jax.ShapeDtypeStruct((FR_DEV, D), f...  37.6 us
    pallas_call x1, Pallas kernels, shards(): pl.pallas_call(halo_kernel, out_shape=(jax.ShapeDtypeStruct((BLOCKS, TILE...  13.5 us
    pallas_call x1, Pallas kernels, shards(): pl.pallas_call(tile_kernel, out_shape=(jax.ShapeDtypeStruct((BLOCKS, TILE...  10 us

profile of v4, /device:TPU:2, one launch (start us, length us, event | category | flops | bytes accessed | tf_op | source)
XLA Modules:
  0.0 63.1 jit_solution(15780061773465612037)
XLA Ops:
  1.3 13.5 %shard_map.167 = (bf16[32,128,32]{2,1,0:T(8,128)(2,1)S(1)}, bf16[40,32,128]{2,1,0:T(8,128)(2,1)S(1)}, bf16[40,128,256]{2,1,0:T(8,128)(2,1)S(1)}, f32[40,1,128]{2...) custom-call(bf16[4096,128]{1,0:T(8,128)(2,1)} %lat_h.1, ...), custom_call_target="tpu_custom_call" | custom-call | tf_op jit(solution)/shard_map/pallas_call | solution.py:415
  14.7 10.0 %shard_map.168 = (f32[32,128,256]{2,1,0:T(8,128)S(1)}, bf16[4096,128]{1,0:T(8,128)(2,1)}, bf16[4096,128]{1,0:T(8,128)(2,1)S(1)}) custom-call(s32[32,128]{1,0:T(8,128)S(1)} %get-tuple-element.16.codes, f32[32,128]{1,0:T(8,128)S(1)} %get-tuple-element.17.lmult, bf16[32,128,32]{2,1,0:T(8,128)(2,1)S(1)} %get-tuple-element.18.A, ...), custom_call_target="tpu_custom_call", output_to_operand_aliasing={{0}: (6, {})} | custom-call | tf_op jit(solution)/shard_map/pallas_call | solution.py:454
  24.8 37.6 %shard_map.169 = f32[128,128]{1,0:T(8,128)S(1)} custom-call(bf16[4096,128]{1,0:T(8,128)(2,1)S(1)} %get-tuple-element.28.upd, f32[2,4096]{1,0:T(2,128)S(1)} %get-tuple-element.29.want), custom_call_target="tpu_custom_call" | custom-call | tf_op jit(solution)/shard_map/pallas_call | solution.py:468
  62.4 0.6 %broadcast_multiply_fusion = f32[128,128]{1,0:T(8,128)} fusion(f32[128,128]{1,0:T(8,128)S(1)} %shard_map.169), kind=kLoop, calls=%fused_computation | loop fusion | flops 16384 | bytes 131072 | tf_op jit(solution)/shard_map/mul | solution.py:489

commit v5 on v4

--- a/solution.py
+++ b/solution.py
@@ -108,7 +108,7 @@
     idx = sr[...].astype(f32)
     idx = jnp.transpose(jnp.concatenate([idx, idx], axis=0))
     lane = lax.broadcasted_iota(i32, (HALO, TILE), 1).astype(f32)
-    for first, pair in ((True, (0, 3)), (False, (1, 2))):
+    for first, pair in ((True, (0,)), (False, (3,)), (False, (1,)), (False, (2,))):
         for p, k in enumerate(pair):
             col = idx[:, k:k + 1]
             high = jnp.floor(col * (1.0 / TILE))
@@ -224,7 +224,6 @@
 
 
 def tile_kernel(codes, lmult, A, B, V, lm, acc_in, lat, w_in, wc2, rows, acc, upd_h, upd, wb, osem):
-    wb[...] = jnp.zeros_like(wb)
     total = lax.fori_loop(0, BLOCKS, lambda r, t: t + codes[r, 127], 0)
 
     def advance(state):
@@ -236,32 +235,43 @@
             out.append(state)
         return out
 
-    def step(it, states):
-        now, last = states[:UNROLL], states[UNROLL:]
-        def distances(q):
-            r, g = now[q]
-            pair = jnp.concatenate([B[codes[r, g * GROUP + u]] for u in range(GROUP)], axis=1)
-            return jnp.dot(A[r], pair, preferred_element_type=f32)
-
-        ahead = distances(0)
+    def weigh(q, r, g, it, sq):
+        off = jnp.where(it * UNROLL + q < total, 0.0, NONE).astype(f32)
+        for u in range(GROUP):
+            level = lm[codes[r, g * GROUP + u]] + (lmult[r, g * GROUP + u] + off)
+            d2 = jnp.maximum(sq[:, u * TILE:(u + 1) * TILE], 1e-12)
+            wb[q, :, u * TILE:(u + 1) * TILE] = jnp.exp2(level - d2 * lax.rsqrt(d2)).astype(bf16)
+
+    def distances(r, g):
+        pair = jnp.concatenate([B[codes[r, g * GROUP + u]] for u in range(GROUP)], axis=1)
+        return jnp.dot(A[r], pair, preferred_element_type=f32)
+
+    def collect(q, r, g):
+        sent = jnp.concatenate([V[codes[r, g * GROUP + u]] for u in range(GROUP)], axis=0)
+        acc[r] = acc[r] + jnp.dot(wb[q], sent, preferred_element_type=f32)
+
+    def step(it, last):
+        now = tuple(advance(last[-1]))
+        ahead = distances(*now[0])
         for q in range(UNROLL):
-            r, g = last[q]
-            sent = jnp.concatenate([V[codes[r, g * GROUP + u]] for u in range(GROUP)], axis=0)
-            acc[r] = acc[r] + jnp.dot(wb[q], sent, preferred_element_type=f32)
+            collect(q, *last[q])
             sq = ahead
             if q + 1 < UNROLL:
-                ahead = distances(q + 1)
-            r, g = now[q]
-            off = jnp.where(it * UNROLL + q < total, 0.0, NONE).astype(f32)
-            for u in range(GROUP):
-                level = lm[codes[r, g * GROUP + u]] + (lmult[r, g * GROUP + u] + off)
-                d2 = jnp.maximum(sq[:, u * TILE:(u + 1) * TILE], 1e-12)
-                wb[q, :, u * TILE:(u + 1) * TILE] = jnp.exp2(level - d2 * lax.rsqrt(d2)).astype(bf16)
-        return tuple(advance(now[-1])) + tuple(now)
+                ahead = distances(*now[q + 1])
+            weigh(q, *now[q], it, sq)
+        return now
 
     zero = jnp.int32(0)
-    first = [(zero, zero)] + advance((zero, zero))[:UNROLL - 1]
-    lax.fori_loop(0, (total + UNROLL - 1) // UNROLL + 1, step, tuple(first) + ((zero, zero),) * UNROLL)
+    first = tuple([(zero, zero)] + advance((zero, zero))[:UNROLL - 1])
+    ahead = distances(*first[0])
+    for q in range(UNROLL):
+        sq = ahead
+        if q + 1 < UNROLL:
+            ahead = distances(*first[q + 1])
+        weigh(q, *first[q], 0, sq)
+    last = lax.fori_loop(1, (total + UNROLL - 1) // UNROLL, step, first)
+    for q in range(UNROLL):
+        collect(q, *last[q])
 
     bias_row = rows[0:1]
     gain_row = rows[1:2]
@@ -435,7 +445,7 @@
             vmem((2, SLOTS), i32), vmem((4, HALO), i32), vmem((128, 32), bf16), vmem((32, 16), bf16),
             vmem((3, D), f32), vmem((D, D), bf16), vmem((1, NODE), i32),
             vmem((16, NODE), f32),
-            vmem((2 * HALO, NODE), bf16),
+            vmem((HALO, NODE), bf16),
             vmem((4, HALO, D), bf16),
             vmem((4, 16, HALO), bf16),
             vmem((4, HALO, D), bf16),

time: 62.7 us -> 62 us (0.989); the launches traced: 63.1 us -> 61.2 us
  Pallas kernels: 61.1 us -> 59.3 us
    pallas_call x1, Pallas kernels: 37.6 us -> 30.8 us  [shards(): pl.pallas_call(pool_kernel, out_shape=jax.ShapeDtypeStruct((FR_DEV, D), f...]
    pallas_call x1, Pallas kernels: 10 us -> 15.7 us  [shards(): pl.pallas_call(tile_kernel, out_shape=(jax.ShapeDtypeStruct((BLOCKS, TILE...]
    pallas_call x1, Pallas kernels: 13.5 us -> 12.8 us  [shards(): pl.pallas_call(halo_kernel, out_shape=(jax.ShapeDtypeStruct((BLOCKS, TILE...]
where the time goes in v5:
time: 62 us; the launch traced here: 61.2 us
  Pallas kernels  59.3 us (96%)
  between operations  1.31 us (2%)
  other arithmetic  0.64 us (1%)
    pallas_call x1, Pallas kernels, shards(): pl.pallas_call(pool_kernel, out_shape=jax.ShapeDtypeStruct((FR_DEV, D), f...  30.8 us
    pallas_call x1, Pallas kernels, shards(): pl.pallas_call(tile_kernel, out_shape=(jax.ShapeDtypeStruct((BLOCKS, TILE...  15.7 us
    pallas_call x1, Pallas kernels, shards(): pl.pallas_call(halo_kernel, out_shape=(jax.ShapeDtypeStruct((BLOCKS, TILE...  12.8 us

profile of v5, /device:TPU:2, one launch (start us, length us, event | category | flops | bytes accessed | tf_op | source)
XLA Modules:
  0.0 61.2 jit_solution(8085925948869445211)
XLA Ops:
  1.3 12.8 %shard_map.167 = (bf16[32,128,32]{2,1,0:T(8,128)(2,1)S(1)}, bf16[40,32,128]{2,1,0:T(8,128)(2,1)S(1)}, bf16[40,128,256]{2,1,0:T(8,128)(2,1)S(1)}, f32[40,1,128]{2...) custom-call(bf16[4096,128]{1,0:T(8,128)(2,1)} %lat_h.1, ...), custom_call_target="tpu_custom_call" | custom-call | tf_op jit(solution)/shard_map/pallas_call | solution.py:425
  14.1 15.7 %shard_map.168 = (f32[32,128,256]{2,1,0:T(8,128)S(1)}, bf16[4096,128]{1,0:T(8,128)(2,1)}, bf16[4096,128]{1,0:T(8,128)(2,1)S(1)}) custom-call(s32[32,128]{1,0:T(8,128)S(1)} %get-tuple-element.16.codes, f32[32,128]{1,0:T(8,128)S(1)} %get-tuple-element.17.lmult, bf16[32,128,32]{2,1,0:T(8,128)(2,1)S(1)} %get-tuple-element.18.A, ...), custom_call_target="tpu_custom_call", output_to_operand_aliasing={{0}: (6, {})} | custom-call | tf_op jit(solution)/shard_map/pallas_call | solution.py:464
  29.8 30.8 %shard_map.169 = f32[128,128]{1,0:T(8,128)S(1)} custom-call(bf16[4096,128]{1,0:T(8,128)(2,1)S(1)} %get-tuple-element.28.upd, f32[2,4096]{1,0:T(2,128)S(1)} %get-tuple-element.29.want), custom_call_target="tpu_custom_call" | custom-call | tf_op jit(solution)/shard_map/pallas_call | solution.py:478
  60.6 0.6 %broadcast_multiply_fusion = f32[128,128]{1,0:T(8,128)} fusion(f32[128,128]{1,0:T(8,128)S(1)} %shard_map.169), kind=kLoop, calls=%fused_computation | loop fusion | flops 16384 | bytes 131072 | tf_op jit(solution)/shard_map/mul | solution.py:499

commit v6 on v5

--- a/solution.py
+++ b/solution.py
@@ -21,7 +21,7 @@
 LOG2E = math.log2(math.e)
 CENTRE = 6.0
 GROUP = 2
-UNROLL = 16
+UNROLL = 20
 NONE = -1e30
 
 f32, bf16, i32 = jnp.float32, jnp.bfloat16, jnp.int32

time: 62 us -> 61.9 us (level); the launches traced: 61.2 us -> 61.8 us
    pallas_call x1, Pallas kernels: 30.8 us -> 36.8 us  [shards(): pl.pallas_call(pool_kernel, out_shape=jax.ShapeDtypeStruct((FR_DEV, D), f...]
    pallas_call x1, Pallas kernels: 15.7 us -> 10.2 us  [shards(): pl.pallas_call(tile_kernel, out_shape=(jax.ShapeDtypeStruct((BLOCKS, TILE...]
where the time goes in v6:
time: 61.9 us; the launch traced here: 61.8 us
  Pallas kernels  59.9 us (97%)
  between operations  1.31 us (2%)
  other arithmetic  0.64 us (1%)
    pallas_call x1, Pallas kernels, shards(): pl.pallas_call(pool_kernel, out_shape=jax.ShapeDtypeStruct((FR_DEV, D), f...  36.8 us
    pallas_call x1, Pallas kernels, shards(): pl.pallas_call(halo_kernel, out_shape=(jax.ShapeDtypeStruct((BLOCKS, TILE...  12.8 us
    pallas_call x1, Pallas kernels, shards(): pl.pallas_call(tile_kernel, out_shape=(jax.ShapeDtypeStruct((BLOCKS, TILE...  10.2 us

profile of v6, /device:TPU:2, one launch (start us, length us, event | category | flops | bytes accessed | tf_op | source)
XLA Modules:
  0.0 61.8 jit_solution(12789478062005800203)
XLA Ops:
  1.3 12.8 %shard_map.167 = (bf16[32,128,32]{2,1,0:T(8,128)(2,1)S(1)}, bf16[40,32,128]{2,1,0:T(8,128)(2,1)S(1)}, bf16[40,128,256]{2,1,0:T(8,128)(2,1)S(1)}, f32[40,1,128]{2...) custom-call(bf16[4096,128]{1,0:T(8,128)(2,1)} %lat_h.1, ...), custom_call_target="tpu_custom_call" | custom-call | tf_op jit(solution)/shard_map/pallas_call | solution.py:425
  14.1 10.2 %shard_map.168 = (f32[32,128,256]{2,1,0:T(8,128)S(1)}, bf16[4096,128]{1,0:T(8,128)(2,1)}, bf16[4096,128]{1,0:T(8,128)(2,1)S(1)}) custom-call(s32[32,128]{1,0:T(8,128)S(1)} %get-tuple-element.16.codes, f32[32,128]{1,0:T(8,128)S(1)} %get-tuple-element.17.lmult, bf16[32,128,32]{2,1,0:T(8,128)(2,1)S(1)} %get-tuple-element.18.A, ...), custom_call_target="tpu_custom_call", output_to_operand_aliasing={{0}: (6, {})} | custom-call | tf_op jit(solution)/shard_map/pallas_call | solution.py:464
  24.3 36.8 %shard_map.169 = f32[128,128]{1,0:T(8,128)S(1)} custom-call(bf16[4096,128]{1,0:T(8,128)(2,1)S(1)} %get-tuple-element.28.upd, f32[2,4096]{1,0:T(2,128)S(1)} %get-tuple-element.29.want), custom_call_target="tpu_custom_call" | custom-call | tf_op jit(solution)/shard_map/pallas_call | solution.py:478
  61.2 0.6 %broadcast_multiply_fusion = f32[128,128]{1,0:T(8,128)} fusion(f32[128,128]{1,0:T(8,128)S(1)} %shard_map.169), kind=kLoop, calls=%fused_computation | loop fusion | flops 16384 | bytes 131072 | tf_op jit(solution)/shard_map/mul | solution.py:499
